TPU v7x, 256 devices: a whole 4x4x8 slice. The times are simulated.
256 devices in a mesh: band: 4 (over x), row: 4 (over y_hi, core), col: 16 (over y_lo, z).
Axes of the slice: x: 4, y: 4 (y_hi: 2, y_lo: 2; y = y_hi * 2 + y_lo), z: 8, core: 2. Of those that a mesh axis runs over, the one named last changes fastest.
Arguments:
- tokens: bfloat16 [256, 32, 16, 1024], P(('band', 'row'), 'col'), may hold values from -10 to 10
- counts: int32 [4], replicated, may hold values from 1 to 4, as said below
- norm_band: bfloat16 [1024], replicated, may hold values from 0.099609375 to 1.8984375
- w_band_qkv: bfloat16 [1024, 1536], replicated, may hold values from -1 to 1
- w_band_out: bfloat16 [512, 1024], replicated, may hold values from -0.25 to 0.25
- norm_space: bfloat16 [1024], replicated, may hold values from 0.099609375 to 1.8984375
- w_space_qkv: bfloat16 [1024, 1536], replicated, may hold values from -1 to 1
- w_space_out: bfloat16 [512, 1024], replicated, may hold values from -0.25 to 0.25
Outputs:
- layer_out: bfloat16 [256, 32, 16, 1024], P(('band', 'row'), 'col')
Inputs may be any that keep to these rules, and one draw needn't show every extreme that they name: `counts`: every group holds at least one live token; some group is full and some group holds exactly one.
All inputs are finite; a program needn't handle non-finite values.
Results may differ from a plain program's by a relative error of at most 0.0063.
Values may be sent and summed in bfloat16 or wider, within the bound.
No kernel may reach another device: no remote copies, remote signals or barrier semaphores. Data moves between devices by JAX's collectives and lax.ppermute only.
A program may use at most 128 MiB of HBM per device.

v0:
```python
import functools

import jax
import jax.numpy as jnp
from jax import lax
from jax.experimental import pallas as pl
from jax.experimental.pallas import tpu as pltpu
from jax.sharding import PartitionSpec as P

HD = 64
HB = 8
HR = 4
HC = 4
EPS = 1e-06
NEG = -1e30
LOG2E = 1.4426950408889634
SCALE2 = HD**-0.5 * LOG2E
F32 = jnp.float32
BF16 = jnp.bfloat16

VMEM = pl.BlockSpec(memory_space=pltpu.VMEM)
SMEM = pl.BlockSpec(memory_space=pltpu.SMEM)
ANY = pl.BlockSpec(memory_space=pl.ANY)


def dot(a, b):
    return jnp.dot(a, b, preferred_element_type=F32)


def dot_t(a, b):
    return lax.dot_general(a, b, (((1,), (1,)), ((), ())), preferred_element_type=F32)


def halves(pair):
    low = lax.broadcasted_iota(jnp.int32, pair.shape, 1) < HD
    zero = jnp.zeros_like(pair)
    return jnp.concatenate([jnp.where(low, pair, zero), jnp.where(low, zero, pair)], axis=0)


def pair_attention(query, keys2, vals2, mask):
    m = query.shape[0]
    n = keys2.shape[0] // 2
    scores = dot_t(query, keys2)
    probs, totals = [], []
    for h in range(2):
        s = scores[:, h * n : (h + 1) * n]
        if mask is not None:
            s = jnp.where(mask, s, NEG)
        p = jnp.exp2((s - jnp.max(s, axis=-1, keepdims=True)) * SCALE2)
        totals.append(jnp.sum(p, axis=-1, keepdims=True))
        probs.append(p.astype(BF16))
    mixed = dot(jnp.concatenate(probs, axis=1), vals2)
    low = lax.broadcasted_iota(jnp.int32, (m, 2 * HD), 1) < HD
    return (mixed / jnp.where(low, totals[0], totals[1])).astype(BF16)


def rms(x, gain):
    scale = lax.rsqrt(jnp.mean(x * x, axis=-1, keepdims=True) + EPS)
    return (x * scale * gain).astype(BF16)


def local_kernel(
    counts, x_ref, g1_ref, g2_ref, w1_hbm, w2_hbm, w3_hbm,
    resid_ref, row_ref, col_ref,
    w1, w2, w3, normed, qkv, heads, wide, sems,
):
    tokens, width = x_ref.shape
    prows, _, _ = row_ref.shape
    slots = col_ref.shape[0]
    pcols = tokens // prows // slots
    inner = HB * HD
    copies = []
    for i in range(3):
        cols = pl.ds(i * inner, inner)
        copies.append(pltpu.make_async_copy(w1_hbm.at[:, cols], w1.at[:, cols], sems.at[i]))
    copies.append(pltpu.make_async_copy(w2_hbm, w2, sems.at[3]))
    for i in range(3):
        cols = pl.ds(i * inner, inner)
        copies.append(pltpu.make_async_copy(w3_hbm.at[:, cols], w3.at[:, cols], sems.at[4 + i]))
    for c in copies:
        c.start()

    g1 = g1_ref[...].astype(F32)
    for b in range(tokens // 64):
        rows = pl.ds(b * 64, 64)
        normed[rows, :] = rms(x_ref[rows, :].astype(F32), g1)
    for i in range(3):
        copies[i].wait()
        for t in range(inner // 256):
            cols = pl.ds(i * inner + t * 256, 256)
            qkv[:, cols] = dot(normed[...], w1[:, cols]).astype(BF16)

    block = 128
    rowi = lax.broadcasted_iota(jnp.int32, (block, block), 0)
    coli = lax.broadcasted_iota(jnp.int32, (block, block), 1)
    slot = coli % slots
    ngroups = counts.shape[0]
    cap = slots // ngroups
    count = jnp.zeros((block, block), jnp.int32)
    for g in range(ngroups):
        count = jnp.where(slot // cap == g, counts[g], count)
    mask = (rowi // slots == coli // slots) & (slot % cap < count)
    for b in range(tokens // block):
        rows = pl.ds(b * block, block)
        for t in range(HB // 2):
            q = qkv[rows, pl.ds(t * 128, 128)]
            k = qkv[rows, pl.ds(inner + t * 128, 128)]
            v = qkv[rows, pl.ds(2 * inner + t * 128, 128)]
            heads[rows, pl.ds(t * 128, 128)] = pair_attention(q, halves(k), halves(v), mask)

    copies[3].wait()
    g2 = g2_ref[...].astype(F32)
    for t in range(width // 256):
        cols = pl.ds(t * 256, 256)
        resid_ref[:, cols] = x_ref[:, cols].astype(F32) + dot(heads[...], w2[:, cols])
    for b in range(tokens // 64):
        rows = pl.ds(b * 64, 64)
        normed[rows, :] = rms(resid_ref[rows, :], g2)

    row_flat = row_ref.shape[1]
    for i in range(3):
        copies[4 + i].wait()
        to = pl.ds(i * 256, 256)
        r = dot(normed[...], w3[:, pl.ds(i * inner, 256)]).astype(BF16)
        row_ref[:, :, to] = r.reshape(prows, row_flat, 256)
        w = dot(normed[...], w3[:, pl.ds(i * inner + 256, 256)])
        wide[0] = w[:, :128]
        wide[1] = w[:, 128:]
        for s in range(slots):
            for c in range(pcols):
                part = [
                    wide[j, pl.ds(c * slots + s, prows, stride=pcols * slots), :]
                    for j in range(2)
                ]
                col_ref[s, pl.ds(c * prows, prows), to] = jnp.concatenate(part, axis=1).astype(BF16)


def row_kernel(x_ref, o_ref, flat):
    n, each, _ = x_ref.shape
    slots = 16
    m = n * each
    block = 128
    rowi = lax.broadcasted_iota(jnp.int32, (block, m), 0)
    coli = lax.broadcasted_iota(jnp.int32, (block, m), 1)
    mask = rowi % slots == coli % slots
    x = x_ref[...].reshape(m, 3 * HR * HD)
    for t in range(HR // 2):
        k = halves(x[:, 256 + t * 128 : 384 + t * 128])
        v = halves(x[:, 512 + t * 128 : 640 + t * 128])
        for b in range(m // block):
            q = x[b * block : (b + 1) * block, t * 128 : (t + 1) * 128]
            flat[pl.ds(b * block, block), pl.ds(t * 128, 128)] = pair_attention(q, k, v, mask)
    o_ref[...] = flat[...].reshape(n, each, HR * HD)


def col_kernel(x_ref, o_ref):
    n, each, _ = x_ref.shape
    prows = 16
    pcols = each // prows
    m = n * prows
    block = 128
    for c in range(pcols):
        part = pl.ds(c * prows, prows)
        for t in range(HC // 2):
            k = halves(x_ref[:, part, pl.ds(256 + t * 128, 128)].reshape(m, 128))
            v = halves(x_ref[:, part, pl.ds(512 + t * 128, 128)].reshape(m, 128))
            for b in range(m // block):
                piece = pl.ds(b * (block // prows), block // prows)
                q = x_ref[piece, part, pl.ds(t * 128, 128)].reshape(block, 128)
                o = pair_attention(q, k, v, None)
                o_ref[piece, part, pl.ds(t * 128, 128)] = o.reshape(block // prows, prows, 128)


def mid_kernel(resid_ref, col_ref, w_ref, acc_ref, wide, natural):
    slots, each, width = col_ref.shape
    prows = 16
    pcols = each // prows
    for j in range(2):
        wide[j] = col_ref[:, :, pl.ds(j * 128, 128)].reshape(slots * each, 128).astype(F32)
    for r in range(prows):
        for c in range(pcols):
            part = [
                wide[j, pl.ds(c * prows + r, slots, stride=each), :]
                for j in range(2)
            ]
            natural[pl.ds((r * pcols + c) * slots, slots), :] = jnp.concatenate(part, axis=1).astype(BF16)
    for t in range(acc_ref.shape[1] // 256):
        cols = pl.ds(t * 256, 256)
        acc_ref[:, cols] = resid_ref[:, cols] + dot(natural[...], w_ref[:, cols])


def last_kernel(acc_ref, row_ref, w_ref, out_ref):
    m = acc_ref.shape[0]
    heads = row_ref[...].reshape(m, row_ref.shape[2])
    for t in range(acc_ref.shape[1] // 256):
        cols = pl.ds(t * 256, 256)
        out_ref[:, cols] = (acc_ref[:, cols] + dot(heads, w_ref[:, cols])).astype(BF16)


def cost(flops, nbytes, trans=0):
    return pl.CostEstimate(flops=flops, bytes_accessed=nbytes, transcendentals=trans)


def local(tokens, counts, norm_band, w_band_qkv, w_band_out, norm_space, w_space_qkv, w_space_out):
    prows, pcols, slots, width = tokens.shape
    m = prows * pcols * slots
    inner = HB * HD
    wide = 3 * HR * HD
    params = pltpu.CompilerParams(vmem_limit_bytes=48 << 20)
    resid, row_qkv, col_qkv = pl.pallas_call(
        local_kernel,
        name="local",
        out_shape=(
            jax.ShapeDtypeStruct((m, width), F32),
            jax.ShapeDtypeStruct((prows, pcols * slots, wide), BF16),
            jax.ShapeDtypeStruct((slots, pcols * prows, wide), BF16),
        ),
        in_specs=[SMEM, VMEM, VMEM, VMEM, ANY, ANY, ANY],
        out_specs=(VMEM, VMEM, VMEM),
        scratch_shapes=[
            pltpu.VMEM(w_band_qkv.shape, BF16),
            pltpu.VMEM(w_band_out.shape, BF16),
            pltpu.VMEM(w_space_qkv.shape, BF16),
            pltpu.VMEM((m, width), BF16),
            pltpu.VMEM((m, 3 * inner), BF16),
            pltpu.VMEM((m, inner), BF16),
            pltpu.VMEM((2, m, 128), F32),
            pltpu.SemaphoreType.DMA((7,)),
        ],
        compiler_params=params,
        cost_estimate=cost(2 * m * width * 4096, 12 << 20),
    )(
        counts, tokens.reshape(m, width), norm_band.reshape(1, width), norm_space.reshape(1, width),
        w_band_qkv, w_band_out, w_space_qkv,
    )
    col_all = lax.all_to_all(col_qkv, ("band", "row"), 0, 0, tiled=True)
    row_all = lax.all_to_all(row_qkv, "col", 0, 0, tiled=True)
    col_o = pl.pallas_call(
        col_kernel,
        name="column_attention",
        out_shape=jax.ShapeDtypeStruct((slots, pcols * prows, HC * HD), BF16),
        in_specs=[VMEM], out_specs=VMEM,
        compiler_params=params,
        cost_estimate=cost(1 << 28, 1 << 20),
    )(col_all)
    row_o = pl.pallas_call(
        row_kernel,
        name="row_attention",
        out_shape=jax.ShapeDtypeStruct((prows, pcols * slots, HR * HD), BF16),
        in_specs=[VMEM], out_specs=VMEM,
        scratch_shapes=[pltpu.VMEM((m, HR * HD), BF16)],
        compiler_params=params,
        cost_estimate=cost(1 << 29, 1 << 20),
    )(row_all)
    col_heads = lax.all_to_all(col_o, ("band", "row"), 0, 0, tiled=True)
    row_heads = lax.all_to_all(row_o, "col", 0, 0, tiled=True)
    acc = pl.pallas_call(
        mid_kernel,
        name="column_projection",
        out_shape=jax.ShapeDtypeStruct((m, width), F32),
        in_specs=[VMEM, VMEM, VMEM], out_specs=VMEM,
        scratch_shapes=[pltpu.VMEM((2, m, 128), F32), pltpu.VMEM((m, HC * HD), BF16)],
        compiler_params=params,
        cost_estimate=cost(2 * m * width * 256, 5 << 20),
    )(resid, col_heads, w_space_out[HR * HD :])
    out = pl.pallas_call(
        last_kernel,
        name="row_projection",
        out_shape=jax.ShapeDtypeStruct((m, width), BF16),
        in_specs=[VMEM, VMEM, VMEM], out_specs=VMEM,
        compiler_params=params,
        cost_estimate=cost(2 * m * width * 256, 5 << 20),
    )(acc, row_heads, w_space_out[: HR * HD])
    return out.reshape(prows, pcols, slots, width)


def solution(mesh):
    placed = (P(("band", "row"), "col", None, None), P(), P(), P(), P(), P(), P(), P())
    return jax.shard_map(
        local,
        mesh=mesh,
        in_specs=placed,
        out_specs=P(("band", "row"), "col", None, None),
        check_vma=False,
    )
```

profile of v0, /device:TPU:32, one launch (start us, length us, event | category | flops | bytes accessed | tf_op | source)
XLA Modules:
  0.0 96.8 jit_solution(18198129247083183171)
XLA Ops:
  0.0 0.7 reshape.13.g1_ref
  0.7 0.7 reshape.14.g2_ref
  1.4 0.0 copy-start.2
  1.4 1.2 %copy-done.2 = bf16[16,2,16,1024]{3,2,1,0:T(8,128)(2,1)S(1)} copy-done((bf16[16,2,16,1024]{3,2,1,0:T(8,128)(2,1)S(1)}, bf16[16,2,16,1024]{3,2,1,0:T(8,128)(2,1)}, u32[]{:S(2)}) %copy-start.2) | copy-done | bytes 1048600
  2.6 0.0 copy-start.3
  2.6 1.2 %copy-done.3 = bf16[512,1024]{1,0:T(8,128)(2,1)S(1)} copy-done((bf16[512,1024]{1,0:T(8,128)(2,1)S(1)}, bf16[512,1024]{1,0:T(8,128)(2,1)}, u32[]{:S(2)}) %copy-start.3) | copy-done | bytes 1048600
  3.8 0.0 copy-start.4
  3.8 0.7 copy-done.4
  4.5 10.0 %local.1 = (f32[512,1024]{1,0:T(8,128)S(1)}, bf16[16,32,768]{2,1,0:T(8,128)(2,1)}, bf16[16,32,768]{2,1,0:T(8,128)(2,1)S(1)}) custom-call(s32[4]{0:T(128)S(1)} %copy-done.4, bf16[512,1024]{1,0:T(8,128)(2,1)S(1)} %bitcast.2, bf16[1,1024]{1,0:T(2,128)(2,1)S(1)} %reshape.13.g1_ref, bf16[1,1024]{1,0:T(2,128)(2,1)S(1)} %reshape.14.g2_ref, ...), custom_call_target="tpu_custom_call" | custom-call | flops 4294967296 | bytes 12582912 | tf_op jit(solution)/shard_map/local/pallas_call | solution.py:210
  14.5 0.0 copy-start
  14.5 1.3 %copy-done = f32[512,1024]{1,0:T(8,128)} copy-done((f32[512,1024]{1,0:T(8,128)}, f32[512,1024]{1,0:T(8,128)S(1)}, u32[]{:S(2)}) %copy-start) | copy-done | bytes 2097176
  15.8 21.6 %all_to_all.20.x_ref = bf16[16,32,768]{2,1,0:T(8,128)(2,1)S(1)} all-to-all(bf16[16,32,768]{2,1,0:T(8,128)(2,1)S(1)} %get-tuple-element.9), channel_id=1, replica_groups=mesh['band'=4,'row'=4,'col'=16] {'band','row'}, dimensions={0} | all-to-all | bytes 1572864 | tf_op jit(solution)/shard_map/all_to_all | solution.py:236
  37.4 0.0 copy-start.5
  37.4 8.8 %all-to-all-start.2 = ((bf16[16,32,768]{2,1,0:T(8,128)(2,1)}), bf16[16,32,768]{2,1,0:T(8,128)(2,1)S(1)}, u32[]{:S(2)}, u32[]{:S(2)}) async-start(bf16[16,32,768]{2,1,0:T(8,128)(2,1)} %get-tuple-element.10), calls=%async_computation.2 | async-start | bytes 1572864 | tf_op jit(solution)/shard_map/all_to_all | solution.py:237
  46.3 2.9 %column_attention.1 = bf16[16,32,256]{2,1,0:T(8,128)(2,1)} custom-call(bf16[16,32,768]{2,1,0:T(8,128)(2,1)S(1)} %all_to_all.20.x_ref), custom_call_target="tpu_custom_call" | custom-call | flops 268435456 | bytes 1048576 | tf_op jit(solution)/shard_map/column_attention/pallas_call | solution.py:238
  49.2 18.0 %all-to-all-done.2.x_ref = bf16[16,32,768]{2,1,0:T(8,128)(2,1)S(1)} async-done(((bf16[16,32,768]{2,1,0:T(8,128)(2,1)}), bf16[16,32,768]{2,1,0:T(8,128)(2,1)S(1)}, u32[]{:S(2)}, u32[]{:S(2)}) %all-to-all-start.2) | async-done | bytes 786464 | tf_op jit(solution)/shard_map/all_to_all | solution.py:237
  67.2 3.6 %all-to-all-start.1 = ((bf16[16,32,256]{2,1,0:T(8,128)(2,1)}), bf16[16,32,256]{2,1,0:T(8,128)(2,1)S(1)}, u32[]{:S(2)}, u32[]{:S(2)}) async-start(bf16[16,32,256]{2,1,0:T(8,128)(2,1)} %column_attention.1), calls=%async_computation.1 | async-start | bytes 524288 | tf_op jit(solution)/shard_map/all_to_all | solution.py:255
  70.8 3.3 %row_attention.1 = bf16[16,32,256]{2,1,0:T(8,128)(2,1)} custom-call(bf16[16,32,768]{2,1,0:T(8,128)(2,1)S(1)} %all-to-all-done.2.x_ref), custom_call_target="tpu_custom_call" | custom-call | flops 536870912 | bytes 1048576 | tf_op jit(solution)/shard_map/row_attention/pallas_call | solution.py:246
  74.1 5.8 %all-to-all-done.1.col_ref = bf16[16,32,256]{2,1,0:T(8,128)(2,1)S(1)} async-done(((bf16[16,32,256]{2,1,0:T(8,128)(2,1)}), bf16[16,32,256]{2,1,0:T(8,128)(2,1)S(1)}, u32[]{:S(2)}, u32[]{:S(2)}) %all-to-all-start.1) | async-done | bytes 262176 | tf_op jit(solution)/shard_map/all_to_all | solution.py:255
  80.0 5.1 %all-to-all-start.3 = ((bf16[16,32,256]{2,1,0:T(8,128)(2,1)}), bf16[16,32,256]{2,1,0:T(8,128)(2,1)S(1)}, u32[]{:S(2)}, u32[]{:S(2)}) async-start(bf16[16,32,256]{2,1,0:T(8,128)(2,1)} %row_attention.1), calls=%async_computation.3 | async-start | bytes 524288 | tf_op jit(solution)/shard_map/all_to_all | solution.py:256
  85.1 0.0 copy-done.5
  85.1 0.1 fusion
  85.2 0.0 copy-start.1
  85.2 1.6 %copy-done.1 = f32[512,1024]{1,0:T(8,128)S(1)} copy-done((f32[512,1024]{1,0:T(8,128)S(1)}, f32[512,1024]{1,0:T(8,128)}, u32[]{:S(2)}) %copy-start.1) | copy-done | bytes 2097176
  86.8 0.7 column_projection.1.acc_ref
  87.5 7.9 %all-to-all-done.3.row_ref = bf16[16,32,256]{2,1,0:T(8,128)(2,1)S(1)} async-done(((bf16[16,32,256]{2,1,0:T(8,128)(2,1)}), bf16[16,32,256]{2,1,0:T(8,128)(2,1)S(1)}, u32[]{:S(2)}, u32[]{:S(2)}) %all-to-all-start.3) | async-done | bytes 262176 | tf_op jit(solution)/shard_map/all_to_all | solution.py:256
  95.4 1.4 %row_projection.1 = bf16[512,1024]{1,0:T(8,128)(2,1)} custom-call(f32[512,1024]{1,0:T(8,128)S(1)} %column_projection.1.acc_ref, bf16[16,32,256]{2,1,0:T(8,128)(2,1)S(1)} %all-to-all-done.3.row_ref, bf16[256,1024]{1,0:T(8,128)(2,1)S(1)} %get-tuple-element.11.w_ref), custom_call_target="tpu_custom_call" | custom-call | flops 268435456 | bytes 5242880 | tf_op jit(solution)/shard_map/row_projection/pallas_call | solution.py:266
Async XLA Ops:
  1.4 1.2 %copy-start.2 = (bf16[16,2,16,1024]{3,2,1,0:T(8,128)(2,1)S(1)}, bf16[16,2,16,1024]{3,2,1,0:T(8,128)(2,1)}, u32[]{:S(2)}) copy-start(bf16[16,2,16,1024]{3,2,1,0:T(8,128)(2,1)} %param.8) | copy-start | bytes 3145732
  2.6 1.2 %copy-start.3 = (bf16[512,1024]{1,0:T(8,128)(2,1)S(1)}, bf16[512,1024]{1,0:T(8,128)(2,1)}, u32[]{:S(2)}) copy-start(bf16[512,1024]{1,0:T(8,128)(2,1)} %w2_hbm.1) | copy-start | bytes 3145732
  3.8 0.7 copy-start.4
  14.5 1.3 %copy-start = (f32[512,1024]{1,0:T(8,128)}, f32[512,1024]{1,0:T(8,128)S(1)}, u32[]{:S(2)}) copy-start(f32[512,1024]{1,0:T(8,128)S(1)} %get-tuple-element.8.resid_ref) | copy-start | bytes 6291460
  37.4 47.7 %copy-start.5 = (bf16[512,1024]{1,0:T(8,128)(2,1)S(1)}, bf16[512,1024]{1,0:T(8,128)(2,1)}, u32[]{:S(2)}) copy-start(bf16[512,1024]{1,0:T(8,128)(2,1)} %param.15) | copy-start | bytes 3145732
  37.4 29.7 %all-to-all-start.2 = ((bf16[16,32,768]{2,1,0:T(8,128)(2,1)}), bf16[16,32,768]{2,1,0:T(8,128)(2,1)S(1)}, u32[]{:S(2)}, u32[]{:S(2)}) async-start(bf16[16,32,768]{2,1,0:T(8,128)(2,1)} %get-tuple-element.10), calls=%async_computation.2 | async-start | bytes 1572864 | tf_op jit(solution)/shard_map/all_to_all | solution.py:237
  67.2 12.8 %all-to-all-start.1 = ((bf16[16,32,256]{2,1,0:T(8,128)(2,1)}), bf16[16,32,256]{2,1,0:T(8,128)(2,1)S(1)}, u32[]{:S(2)}, u32[]{:S(2)}) async-start(bf16[16,32,256]{2,1,0:T(8,128)(2,1)} %column_attention.1), calls=%async_computation.1 | async-start | bytes 524288 | tf_op jit(solution)/shard_map/all_to_all | solution.py:255
  80.0 15.4 %all-to-all-start.3 = ((bf16[16,32,256]{2,1,0:T(8,128)(2,1)}), bf16[16,32,256]{2,1,0:T(8,128)(2,1)S(1)}, u32[]{:S(2)}, u32[]{:S(2)}) async-start(bf16[16,32,256]{2,1,0:T(8,128)(2,1)} %row_attention.1), calls=%async_computation.3 | async-start | bytes 524288 | tf_op jit(solution)/shard_map/all_to_all | solution.py:256
  85.2 1.6 %copy-start.1 = (f32[512,1024]{1,0:T(8,128)S(1)}, f32[512,1024]{1,0:T(8,128)}, u32[]{:S(2)}) copy-start(f32[512,1024]{1,0:T(8,128)} %copy-done) | copy-start | bytes 6291460
where the time goes:
time: 97.3 us; the launch traced here: 96.8 us
  waiting for transfers between devices  31.7 us (33%)
  blocking collectives  21.6 us (22%)
  Pallas kernels  18.4 us (19%)
  starting transfers between devices  17.6 us (18%)
  local copies, waits for them, and re-layouts  7.45 us (8%)
    all_to_all x1, blocking collectives, local(): col_all = lax.all_to_all(col_qkv, ('band', 'row'), 0, 0, tiled=True)  21.6 us
    all_to_all x1, waiting for transfers between devices, local(): row_all = lax.all_to_all(row_qkv, 'col', 0, 0, tiled=True)  18 us
    pallas_call x1, Pallas kernels, local(): pl.pallas_call(local_kernel, name='local', out_shape=(jax.ShapeDtypeStruc...  10 us
    all_to_all x1, starting transfers between devices, local(): row_all = lax.all_to_all(row_qkv, 'col', 0, 0, tiled=True)  8.83 us
    all_to_all x1, waiting for transfers between devices, local(): row_heads = lax.all_to_all(row_o, 'col', 0, 0, tiled=True)  7.91 us
    unnamed x12, local copies, waits for them, and re-layouts  6.01 us
    all_to_all x1, waiting for transfers between devices, local(): col_heads = lax.all_to_all(col_o, ('band', 'row'), 0, 0, tiled=True)  5.84 us
    all_to_all x1, starting transfers between devices, local(): row_heads = lax.all_to_all(row_o, 'col', 0, 0, tiled=True)  5.13 us
  transfers between devices with their start and end apart: 3, of which 3 were waited for; matrix products, arithmetic and copies ran while one was open for 0% of the time, Pallas kernels for 7%

commit v1 on v0

v1 whole, which is shorter than its diff:
```python
import jax
import jax.numpy as jnp
from jax import lax
from jax.experimental import pallas as pl
from jax.experimental.pallas import tpu as pltpu
from jax.sharding import PartitionSpec as P


HD = 64
HB = 8
HR = 4
HC = 4
EPS = 1e-06
NEG = -1e30
LOG2E = 1.4426950408889634
SCALE2 = HD**-0.5 * LOG2E
F32 = jnp.float32
BF16 = jnp.bfloat16

VMEM = pl.BlockSpec(memory_space=pltpu.VMEM)
SMEM = pl.BlockSpec(memory_space=pltpu.SMEM)
HBM = pl.BlockSpec(memory_space=pltpu.HBM)


def dot(a, b):
    return jnp.dot(a, b, preferred_element_type=F32)


def dot_t(a, b):
    return lax.dot_general(a, b, (((1,), (1,)), ((), ())), preferred_element_type=F32)


def halves(pair):
    low = lax.broadcasted_iota(jnp.int32, pair.shape, 1) < HD
    zero = jnp.zeros_like(pair)
    return jnp.concatenate([jnp.where(low, pair, zero), jnp.where(low, zero, pair)], axis=0)


def pair_attention(query, keys2, vals2, mask):
    m = query.shape[0]
    n = keys2.shape[0] // 2
    scores = dot_t(query, keys2)
    probs, totals = [], []
    for h in range(2):
        s = scores[:, h * n : (h + 1) * n]
        if mask is not None:
            s = jnp.where(mask, s, NEG)
        p = jnp.exp2((s - jnp.max(s, axis=-1, keepdims=True)) * SCALE2)
        totals.append(jnp.sum(p, axis=-1, keepdims=True))
        probs.append(p.astype(BF16))
    mixed = dot(jnp.concatenate(probs, axis=1), vals2)
    low = lax.broadcasted_iota(jnp.int32, (m, 2 * HD), 1) < HD
    return (mixed / jnp.where(low, totals[0], totals[1])).astype(BF16)


def rms(x, gain):
    scale = lax.rsqrt(jnp.mean(x * x, axis=-1, keepdims=True) + EPS)
    return (x * scale * gain).astype(BF16)


def local_kernel(
    counts_hbm, x_hbm, g1_hbm, g2_hbm, w1_hbm, w2_hbm, w3_hbm,
    resid_hbm, normed_ref, row_ref,
    counts, x_ref, g1_ref, g2_ref, w1, w2, w3, normed, qkv, heads, resid_ref, sems, wsems, rsems,
):
    prows, row_flat, _ = row_ref.shape
    tokens, width = resid_ref.shape
    slots = x_hbm.shape[2]
    inner = HB * HD
    small = [
        pltpu.make_async_copy(counts_hbm, counts, sems.at[0]),
        pltpu.make_async_copy(g1_hbm, g1_ref, sems.at[1]),
        pltpu.make_async_copy(g2_hbm, g2_ref, sems.at[2]),
    ]
    quarter = prows // 4
    loads = [
        pltpu.make_async_copy(
            x_hbm.at[pl.ds(i * quarter, quarter)], x_ref.at[pl.ds(i * quarter, quarter)], sems.at[3 + i]
        )
        for i in range(4)
    ]
    copies = []
    for i in range(3):
        cols = pl.ds(i * inner, inner)
        copies.append(pltpu.make_async_copy(w1_hbm.at[:, cols], w1.at[:, cols], wsems.at[i]))
    copies.append(pltpu.make_async_copy(w2_hbm, w2, wsems.at[3]))
    for i in range(3):
        copies.append(
            pltpu.make_async_copy(
                w3_hbm.at[:, pl.ds(i * inner, 256)], w3.at[:, pl.ds(i * 256, 256)], wsems.at[4 + i]
            )
        )
    for c in small + loads + copies:
        c.start()

    small[1].wait()
    g1 = g1_ref[...].astype(F32).reshape(1, width)
    chunk = tokens // 8
    for b in range(8):
        if b % 2 == 0:
            loads[b // 2].wait()
        rows = pl.ds(b * chunk, chunk)
        x = x_ref[pl.ds(b * prows // 8, prows // 8)].reshape(chunk, width)
        normed[rows, :] = rms(x.astype(F32), g1)
    for i in range(3):
        copies[i].wait()
        for t in range(inner // 256):
            cols = pl.ds(i * inner + t * 256, 256)
            qkv[:, cols] = dot(normed[...], w1[:, cols]).astype(BF16)

    small[0].wait()
    block = 128
    rowi = lax.broadcasted_iota(jnp.int32, (block, block), 0)
    coli = lax.broadcasted_iota(jnp.int32, (block, block), 1)
    slot = coli % slots
    ngroups = counts.shape[0]
    cap = slots // ngroups
    count = jnp.zeros((block, block), jnp.int32)
    for g in range(ngroups):
        count = jnp.where(slot // cap == g, counts[g], count)
    mask = (rowi // slots == coli // slots) & (slot % cap < count)
    for b in range(tokens // block):
        rows = pl.ds(b * block, block)
        for t in range(HB // 2):
            q = qkv[rows, pl.ds(t * 128, 128)]
            k = qkv[rows, pl.ds(inner + t * 128, 128)]
            v = qkv[rows, pl.ds(2 * inner + t * 128, 128)]
            heads[rows, pl.ds(t * 128, 128)] = pair_attention(q, halves(k), halves(v), mask)

    copies[3].wait()
    small[2].wait()
    g2 = g2_ref[...].astype(F32).reshape(1, width)
    for t in range(width // 256):
        cols = pl.ds(t * 256, 256)
        x = x_ref[:, :, :, cols].reshape(tokens, 256)
        resid_ref[:, cols] = x.astype(F32) + dot(heads[...], w2[:, cols])
    stores = [
        pltpu.make_async_copy(
            resid_ref.at[pl.ds(i * 128, 128)], resid_hbm.at[pl.ds(i * 128, 128)], rsems.at[i]
        )
        for i in range(tokens // 128)
    ]
    for c in stores:
        c.start()
    for b in range(8):
        rows = pl.ds(b * chunk, chunk)
        normed_ref[rows, :] = rms(resid_ref[rows, :], g2)

    for i in range(3):
        copies[4 + i].wait()
        to = pl.ds(i * 256, 256)
        r = dot(normed_ref[...], w3[:, to]).astype(BF16)
        row_ref[:, :, to] = r.reshape(prows, row_flat, 256)
    for c in stores:
        c.wait()


def column_qkv_kernel(me_ref, normed_ref, w3_hbm, keep_ref, send_ref, w3, wide, wsems):
    slots = 2 * keep_ref.shape[0]
    prows = slots
    pcols = keep_ref.shape[1] // prows
    inner = HB * HD
    me = me_ref[0]
    copies = [
        pltpu.make_async_copy(
            w3_hbm.at[:, pl.ds(i * inner + 256, 256)], w3.at[:, pl.ds(i * 256, 256)], wsems.at[i]
        )
        for i in range(3)
    ]
    for c in copies:
        c.start()
    for i in range(3):
        copies[i].wait()
        to = pl.ds(i * 256, 256)
        w = dot(normed_ref[...], w3[:, to])
        wide[i % 2, 0] = w[:, :128]
        wide[i % 2, 1] = w[:, 128:]
        for d in range(slots):
            ref = send_ref if d % 2 else keep_ref
            s = me ^ d
            for c in range(pcols):
                part = [
                    wide[i % 2, j, pl.ds(c * slots + s, prows, stride=pcols * slots), :]
                    for j in range(2)
                ]
                ref[d // 2, pl.ds(c * prows, prows), to] = jnp.concatenate(part, axis=1).astype(BF16)


def row_kernel(x_ref, o_ref, flat):
    n, each, _ = x_ref.shape
    slots = 16
    m = n * each
    block = 128
    rowi = lax.broadcasted_iota(jnp.int32, (block, m), 0)
    coli = lax.broadcasted_iota(jnp.int32, (block, m), 1)
    mask = rowi % slots == coli % slots
    x = x_ref[...].reshape(m, 3 * HR * HD)
    for t in range(HR // 2):
        k = halves(x[:, 256 + t * 128 : 384 + t * 128])
        v = halves(x[:, 512 + t * 128 : 640 + t * 128])
        for b in range(m // block):
            q = x[b * block : (b + 1) * block, t * 128 : (t + 1) * 128]
            flat[pl.ds(b * block, block), pl.ds(t * 128, 128)] = pair_attention(q, k, v, mask)
    o_ref[...] = flat[...].reshape(n, each, HR * HD)


def col_kernel(keep_ref, cross_ref, *refs):
    n = len(refs) // 2
    pieces, outs = refs[: n], refs[n:]
    prows = 16
    each, _ = keep_ref.shape[1:]
    pcols = each // prows
    views = [(keep_ref.at[0], cross_ref.at[0])] + [(p.at[0], p.at[1]) for p in pieces]
    flat = [v for pair in views for v in pair]
    for c in range(pcols):
        part = pl.ds(c * prows, prows)

        def take(refs_, at):
            return jnp.concatenate([r[part, pl.ds(at, 128)] for r in refs_], axis=0)

        for t in range(HC // 2):
            k = halves(take(flat, 256 + t * 128))
            v = halves(take(flat, 512 + t * 128))
            for b in range(len(flat) // 8):
                q = take(flat[b * 8 : b * 8 + 8], t * 128)
                o = pair_attention(q, k, v, None)
                for i in range(8):
                    p = b * 8 + i
                    outs[p // 2][p % 2, part, pl.ds(t * 128, 128)] = o[i * prows : (i + 1) * prows]


def mid_kernel(me_ref, resid_hbm, cross_ref, *refs):
    pieces, (w_ref, acc_ref, wide, natural, resid_ref, rsems) = refs[:8], refs[8:]
    loads = []
    for t in range(acc_ref.shape[1] // 256):
        cols = pl.ds(t * 256, 256)
        loads.append(pltpu.make_async_copy(resid_hbm.at[:, cols], resid_ref.at[:, cols], rsems.at[t]))
        loads[t].start()
    slots = 2 * len(pieces)
    each = cross_ref.shape[1]
    prows = 16
    pcols = each // prows
    me = me_ref[0]
    for d in range(slots):
        piece = cross_ref.at[d // 2] if d % 2 else pieces[d // 2].at[0]
        to = pl.ds(pl.multiple_of((me ^ d) * each, each), each)
        for j in range(2):
            wide[j, to, :] = piece[:, pl.ds(j * 128, 128)].astype(F32)
    for r in range(prows):
        for c in range(pcols):
            part = [wide[j, pl.ds(c * prows + r, slots, stride=each), :] for j in range(2)]
            natural[pl.ds((r * pcols + c) * slots, slots), :] = jnp.concatenate(part, axis=1).astype(BF16)
    for t in range(acc_ref.shape[1] // 256):
        cols = pl.ds(t * 256, 256)
        loads[t].wait()
        acc_ref[:, cols] = resid_ref[:, cols] + dot(natural[...], w_ref[:, cols])


def last_kernel(acc_ref, row_ref, w_ref, out_ref):
    m = acc_ref.shape[0]
    heads = row_ref[...].reshape(m, row_ref.shape[2])
    for t in range(acc_ref.shape[1] // 256):
        cols = pl.ds(t * 256, 256)
        out_ref[:, cols] = (acc_ref[:, cols] + dot(heads, w_ref[:, cols])).astype(BF16)


def cost(flops, nbytes, trans=0):
    return pl.CostEstimate(flops=flops, bytes_accessed=nbytes, transcendentals=trans)


def flip(array, axes, n, by):
    return lax.ppermute(array, axes, [(i, i ^ by) for i in range(n)])


def local(tokens, counts, norm_band, w_band_qkv, w_band_out, norm_space, w_space_qkv, w_space_out):
    prows, pcols, slots, width = tokens.shape
    m = prows * pcols * slots
    inner = HB * HD
    wide = 3 * HR * HD
    half = slots // 2
    each = pcols * prows
    rows_axes = ("band", "row")
    me = lax.axis_index(rows_axes).astype(jnp.int32).reshape(1)

    def params(mib):
        return pltpu.CompilerParams(vmem_limit_bytes=mib << 20)

    resid, normed, row_qkv = pl.pallas_call(
        local_kernel,
        name="local",
        out_shape=(
            jax.ShapeDtypeStruct((m, width), F32),
            jax.ShapeDtypeStruct((m, width), BF16),
            jax.ShapeDtypeStruct((prows, pcols * slots, wide), BF16),
        ),
        in_specs=[HBM] * 7,
        out_specs=(HBM, VMEM, VMEM),
        scratch_shapes=[
            pltpu.SMEM(counts.shape, jnp.int32),
            pltpu.VMEM(tokens.shape, BF16),
            pltpu.VMEM((width,), BF16),
            pltpu.VMEM((width,), BF16),
            pltpu.VMEM(w_band_qkv.shape, BF16),
            pltpu.VMEM(w_band_out.shape, BF16),
            pltpu.VMEM((width, wide), BF16),
            pltpu.VMEM((m, width), BF16),
            pltpu.VMEM((m, 3 * inner), BF16),
            pltpu.VMEM((m, inner), BF16),
            pltpu.VMEM((m, width), F32),
            pltpu.SemaphoreType.DMA((7,)),
            pltpu.SemaphoreType.DMA((7,)),
            pltpu.SemaphoreType.DMA((m // 128,)),
        ],
        compiler_params=params(59),
        cost_estimate=cost(2 * m * width * 3300, 12 << 20),
    )(counts, tokens, norm_band, norm_space, w_band_qkv, w_band_out, w_space_qkv)
    row_all = lax.all_to_all(row_qkv, "col", 0, 0, tiled=True)
    keep, send = pl.pallas_call(
        column_qkv_kernel,
        name="column_qkv",
        out_shape=(jax.ShapeDtypeStruct((half, each, wide), BF16),) * 2,
        in_specs=[SMEM, VMEM, HBM],
        out_specs=(VMEM, VMEM),
        scratch_shapes=[
            pltpu.VMEM((width, wide), BF16),
            pltpu.VMEM((2, 2, m, 128), F32),
            pltpu.SemaphoreType.DMA((3,)),
        ],
        compiler_params=params(16),
        cost_estimate=cost(2 * m * width * wide, 4 << 20),
    )(me, normed, w_space_qkv)
    cross = flip(send, rows_axes, slots, 1)
    got = []
    for d in range(1, half):
        got.append(flip(jnp.stack([keep[d], cross[d]]), rows_axes, slots, 2 * d))

    col_o = pl.pallas_call(
        col_kernel,
        name="column_attention",
        out_shape=(jax.ShapeDtypeStruct((2, each, HC * HD), BF16),) * half,
        in_specs=[VMEM] * (half + 1),
        out_specs=(VMEM,) * half,
        compiler_params=params(16),
        cost_estimate=cost(1 << 28, 1 << 20),
    )(keep, cross, *got)
    row_o = pl.pallas_call(
        row_kernel,
        name="row_attention",
        out_shape=jax.ShapeDtypeStruct((prows, pcols * slots, HR * HD), BF16),
        in_specs=[VMEM], out_specs=VMEM,
        scratch_shapes=[pltpu.VMEM((m, HR * HD), BF16)],
        compiler_params=params(16),
        cost_estimate=cost(1 << 29, 1 << 20),
    )(row_all)
    row_heads = lax.all_to_all(row_o, "col", 0, 0, tiled=True)
    back = [col_o[0]]
    for d in range(1, half):
        back.append(flip(col_o[d], rows_axes, slots, 2 * d))
    cross_back = flip(jnp.stack([b[1] for b in back]), rows_axes, slots, 1)
    acc = pl.pallas_call(
        mid_kernel,
        name="column_projection",
        out_shape=jax.ShapeDtypeStruct((m, width), F32),
        in_specs=[SMEM, HBM, VMEM] + [VMEM] * half + [VMEM], out_specs=VMEM,
        scratch_shapes=[
            pltpu.VMEM((2, m, 128), F32),
            pltpu.VMEM((m, HC * HD), BF16),
            pltpu.VMEM((m, width), F32),
            pltpu.SemaphoreType.DMA((width // 256,)),
        ],
        compiler_params=params(56),
        cost_estimate=cost(2 * m * width * 256, 5 << 20),
    )(me, resid, cross_back, *back, w_space_out[HR * HD :])
    out = pl.pallas_call(
        last_kernel,
        name="row_projection",
        out_shape=jax.ShapeDtypeStruct((m, width), BF16),
        in_specs=[VMEM, VMEM, VMEM], out_specs=VMEM,
        compiler_params=params(16),
        cost_estimate=cost(2 * m * width * 256, 5 << 20),
    )(acc, row_heads, w_space_out[: HR * HD])
    return out.reshape(prows, pcols, slots, width)


def solution(mesh):
    placed = (P(("band", "row"), "col", None, None), P(), P(), P(), P(), P(), P(), P())
    return jax.shard_map(
        local,
        mesh=mesh,
        in_specs=placed,
        out_specs=P(("band", "row"), "col", None, None),
        check_vma=False,
    )
```

time: 97.3 us -> 86.3 us (0.89)
  starting transfers between devices: 17.6 us -> 45.5 us
  waiting for transfers between devices: 31.7 us -> 6.63 us
  blocking collectives: 21.6 us -> 0 us
  Pallas kernels: 18.4 us -> 26.6 us
  local copies, waits for them, and re-layouts: 7.45 us -> 4.38 us
  other arithmetic: 0 us -> 2.62 us
    ppermute x0 -> x16, starting transfers between devices: none -> 29 us  [flip(): return lax.ppermute(array, axes, [(i, i ^ by) for i in range(n)])]
    all_to_all x1 -> x0, blocking collectives: 21.6 us -> none  [local(): col_all = lax.all_to_all(col_qkv, ('band', 'row'), 0, 0, tiled=True)]
    all_to_all x1, waiting for transfers between devices: 18 us -> 0.66 us  [local(): row_all = lax.all_to_all(row_qkv, 'col', 0, 0, tiled=True)]
    all_to_all x1 -> x0, waiting for transfers between devices: 5.84 us -> none  [local(): col_heads = lax.all_to_all(col_o, ('band', 'row'), 0, 0, tiled=True)]
    all_to_all x1, waiting for transfers between devices: 7.91 us -> 2.12 us  [local(): row_heads = lax.all_to_all(row_o, 'col', 0, 0, tiled=True)]
    pallas_call x1, Pallas kernels: 0.69 us -> 4.8 us  [local(): pl.pallas_call(mid_kernel, name='column_projection', out_shape=jax.ShapeD...]
    ppermute x0 -> x16, waiting for transfers between devices: none -> 3.85 us  [flip(): return lax.ppermute(array, axes, [(i, i ^ by) for i in range(n)])]
    all_to_all x1 -> x0, starting transfers between devices: 3.61 us -> none  [local(): col_heads = lax.all_to_all(col_o, ('band', 'row'), 0, 0, tiled=True)]
  transfers between devices with their start and end apart: 3 -> 18, of which waited for: 3 -> 6; matrix products, arithmetic and copies ran while one was open for 0% -> 4% of each run, Pallas kernels for 7% -> 12%
where the time goes in v1:
time: 86.3 us; the launch traced here: 86 us
  starting transfers between devices  45.5 us (53%)
  Pallas kernels  26.6 us (31%)
  waiting for transfers between devices  6.63 us (8%)
  local copies, waits for them, and re-layouts  4.38 us (5%)
  other arithmetic  2.62 us (3%)
    ppermute x16, starting transfers between devices, flip(): return lax.ppermute(array, axes, [(i, i ^ by) for i in range(n)])  29 us
    pallas_call x1, Pallas kernels, local(): pl.pallas_call(local_kernel, name='local', out_shape=(jax.ShapeDtypeStruc...  12 us
    all_to_all x1, starting transfers between devices, local(): row_all = lax.all_to_all(row_qkv, 'col', 0, 0, tiled=True)  9.6 us
    all_to_all x1, starting transfers between devices, local(): row_heads = lax.all_to_all(row_o, 'col', 0, 0, tiled=True)  6.87 us
    pallas_call x1, Pallas kernels, local(): pl.pallas_call(mid_kernel, name='column_projection', out_shape=jax.ShapeD...  4.8 us
    ppermute x16, waiting for transfers between devices, flip(): return lax.ppermute(array, axes, [(i, i ^ by) for i in range(n)])  3.85 us
    unnamed x33, local copies, waits for them, and re-layouts  3.46 us
    pallas_call x1, Pallas kernels, local(): pl.pallas_call(row_kernel, name='row_attention', out_shape=jax.ShapeDtype...  3.36 us
  transfers between devices with their start and end apart: 18, of which 6 were waited for; matrix products, arithmetic and copies ran while one was open for 4% of the time, Pallas kernels for 12%

profile of v1, /device:TPU:32, one launch (start us, length us, event | category | flops | bytes accessed | tf_op | source)
XLA Modules:
  0.0 86.0 jit_solution(6159360998919279221)
XLA Ops:
  0.0 12.0 %local.1 = (f32[512,1024]{1,0:T(8,128)}, bf16[512,1024]{1,0:T(8,128)(2,1)}, bf16[16,32,768]{2,1,0:T(8,128)(2,1)}) custom-call(s32[4]{0:T(128)} %counts_hbm.1, bf16[16,2,16,1024]{3,2,1,0:T(8,128)(2,1)} %x_hbm.1, bf16[1024]{0:T(1024)(128)(2,1)} %g1_hbm.1, bf16[1024]{0:T(1024)(128)(2,1)} %g2_hbm.1, bf16[1024,1536]{1,0:T(8,128)(2,1)} %w1_hbm.1, ...), custom_call_target="tpu_custom_call" | custom-call | flops 3460300800 | bytes 12582912 | tf_op jit(solution)/shard_map/local/pallas_call | solution.py:288
  12.0 0.0 copy-start.2
  12.0 1.2 %copy-done.2 = bf16[512,1024]{1,0:T(8,128)(2,1)S(1)} copy-done((bf16[512,1024]{1,0:T(8,128)(2,1)S(1)}, bf16[512,1024]{1,0:T(8,128)(2,1)}, u32[]{:S(2)}) %copy-start.2) | copy-done | bytes 1048600
  13.2 2.8 %column_qkv.1 = (bf16[8,32,768]{2,1,0:T(8,128)(2,1)S(1)}, bf16[8,32,768]{2,1,0:T(8,128)(2,1)S(1)}) custom-call(s32[1]{0:T(128)} %bitcast.me_ref, bf16[512,1024]{1,0:T(8,128)(2,1)S(1)} %copy-done.2, bf16[1024,1536]{1,0:T(8,128)(2,1)S(1)} %copy-done.1), custom_call_target="tpu_custom_call" | custom-call | flops 805306368 | bytes 4194304 | tf_op jit(solution)/shard_map/column_qkv/pallas_call | solution.py:318
  16.0 0.1 collective-permute-start
  16.2 1.7 %collective-permute-done.cross_ref = bf16[8,32,768]{2,1,0:T(8,128)(2,1)S(1)} collective-permute-done((bf16[8,32,768]{2,1,0:T(8,128)(2,1)S(1)}, bf16[8,32,768]{2,1,0:T(8,128)(2,1)S(1)}, u32[]{:S(2)}, u32[]{:S(2)}) %collective-permute-start) | collective-permute-done | bytes 393248 | tf_op jit(solution)/shard_map/ppermute | solution.py:272
  17.9 3.3 %collective-permute-start.1 = (bf16[2,32,768]{2,1,0:T(8,128)(2,1)S(1)}, bf16[2,32,768]{2,1,0:T(8,128)(2,1)S(1)}, u32[]{:S(2)}, u32[]{:S(2)}) collective-permute-start(bf16[2,32,768]{2,1,0:T(8,128)(2,1)S(1)} %pad_maximum_fusion), channel_id=1, source_target_pairs={{0,32},{16,48},{32,0},{48,16},{64,96},{80,112},{96,64},{112,80},{1... | collective-permute-start | bytes 294920 | tf_op jit(solution)/shard_map/ppermute | solution.py:272
  21.2 1.6 %collective-permute-start.2 = (bf16[2,32,768]{2,1,0:T(8,128)(2,1)S(1)}, bf16[2,32,768]{2,1,0:T(8,128)(2,1)S(1)}, u32[]{:S(2)}, u32[]{:S(2)}) collective-permute-start(bf16[2,32,768]{2,1,0:T(8,128)(2,1)S(1)} %pad_maximum_fusion.1), channel_id=1, source_target_pairs={{0,64},{16,80},{32,96},{48,112},{64,0},{80,16},{96,32},{112,48},{1... | collective-permute-start | bytes 294920 | tf_op jit(solution)/shard_map/ppermute | solution.py:272
  22.8 0.4 collective-permute-start.3
  23.2 0.7 pad_maximum_fusion.3
  23.8 3.0 %collective-permute-start.4 = (bf16[2,32,768]{2,1,0:T(8,128)(2,1)}, bf16[2,32,768]{2,1,0:T(8,128)(2,1)S(1)}, u32[]{:S(2)}, u32[]{:S(2)}) collective-permute-start(bf16[2,32,768]{2,1,0:T(8,128)(2,1)} %pad_maximum_fusion.3), channel_id=1, source_target_pairs={{0,128},{16,144},{32,160},{48,176},{64,192},{80,208},{96,224},{112... | collective-permute-start | bytes 294920 | tf_op jit(solution)/shard_map/ppermute | solution.py:272
  26.9 0.6 pad_maximum_fusion.4
  27.5 3.1 %collective-permute-start.5 = (bf16[2,32,768]{2,1,0:T(8,128)(2,1)}, bf16[2,32,768]{2,1,0:T(8,128)(2,1)S(1)}, u32[]{:S(2)}, u32[]{:S(2)}) collective-permute-start(bf16[2,32,768]{2,1,0:T(8,128)(2,1)} %pad_maximum_fusion.4), channel_id=1, source_target_pairs={{0,160},{16,176},{32,128},{48,144},{64,224},{80,240},{96,192},{112... | collective-permute-start | bytes 294920 | tf_op jit(solution)/shard_map/ppermute | solution.py:272
  30.6 0.6 pad_maximum_fusion.6
  31.3 0.6 pad_maximum_fusion.5
  31.9 0.0 collective-permute-done.1.refs_0_
  31.9 2.8 %collective-permute-start.6 = (bf16[2,32,768]{2,1,0:T(8,128)(2,1)}, bf16[2,32,768]{2,1,0:T(8,128)(2,1)S(1)}, u32[]{:S(2)}, u32[]{:S(2)}) collective-permute-start(bf16[2,32,768]{2,1,0:T(8,128)(2,1)} %pad_maximum_fusion.5), channel_id=1, source_target_pairs={{0,192},{16,208},{32,224},{48,240},{64,128},{80,144},{96,160},{112... | collective-permute-start | bytes 294920 | tf_op jit(solution)/shard_map/ppermute | solution.py:272
  34.7 0.0 collective-permute-done.2.refs_1_
  34.7 0.2 collective-permute-start.7
  35.0 9.6 %all-to-all-start = ((bf16[16,32,768]{2,1,0:T(8,128)(2,1)}), bf16[16,32,768]{2,1,0:T(8,128)(2,1)S(1)}, u32[]{:S(2)}, u32[]{:S(2)}) async-start(bf16[16,32,768]{2,1,0:T(8,128)(2,1)} %get-tuple-element.30), calls=%async_computation | async-start | bytes 1572864 | tf_op jit(solution)/shard_map/all_to_all | solution.py:317
  44.6 0.0 collective-permute-done.4.refs_3_
  44.6 0.0 collective-permute-done.5.refs_4_
  44.6 0.0 collective-permute-done.7.refs_6_
  44.6 2.2 %column_attention.1 = (bf16[2,32,256]{2,1,0:T(8,128)(2,1)S(1)}, bf16[2,32,256]{2,1,0:T(8,128)(2,1)S(1)}, bf16[2,32,256]{2,1,0:T(8,128)(2,1)S(1)}, bf16[2,32,256]...) custom-call(bf16[8,32,768]{2,1,0:T(8,128)(2,1)S(1)} %get-tuple-eleme, ...), custom_call_target="tpu_custom_call" | custom-call | flops 268435456 | bytes 1048576 | tf_op jit(solution)/shard_map/column_attention/pallas_call | solution.py:337
  46.8 3.0 %collective-permute-start.8 = (bf16[2,32,256]{2,1,0:T(8,128)(2,1)S(1)}, bf16[2,32,256]{2,1,0:T(8,128)(2,1)S(1)}, u32[]{:S(2)}, u32[]{:S(2)}) collective-permute-start(bf16[2,32,256]{2,1,0:T(8,128)(2,1)S(1)} %get-tuple-element.23), channel_id=1, source_target_pairs={{0,32},{16,48},{32,0},{48,16},{64,96},{80,112},{96,64},{112,80},{1... | collective-permute-start | bytes 98312 | tf_op jit(solution)/shard_map/ppermute | solution.py:272
  49.8 0.3 collective-permute-start.9
  50.1 1.8 %collective-permute-start.10 = (bf16[2,32,256]{2,1,0:T(8,128)(2,1)S(1)}, bf16[2,32,256]{2,1,0:T(8,128)(2,1)S(1)}, u32[]{:S(2)}, u32[]{:S(2)}) collective-permute-start(bf16[2,32,256]{2,1,0:T(8,128)(2,1)S(1)} %get-tuple-element.25), channel_id=1, source_target_pairs={{0,96},{16,112},{32,64},{48,80},{64,32},{80,48},{96,0},{112,16},{1... | collective-permute-start | bytes 98312 | tf_op jit(solution)/shard_map/ppermute | solution.py:272
  51.9 2.2 %collective-permute-start.11 = (bf16[2,32,256]{2,1,0:T(8,128)(2,1)S(1)}, bf16[2,32,256]{2,1,0:T(8,128)(2,1)S(1)}, u32[]{:S(2)}, u32[]{:S(2)}) collective-permute-start(bf16[2,32,256]{2,1,0:T(8,128)(2,1)S(1)} %get-tuple-element.26), channel_id=1, source_target_pairs={{0,128},{16,144},{32,160},{48,176},{64,192},{80,208},{96,224},{112... | collective-permute-start | bytes 98312 | tf_op jit(solution)/shard_map/ppermute | solution.py:272
  54.1 3.7 %collective-permute-start.12 = (bf16[2,32,256]{2,1,0:T(8,128)(2,1)S(1)}, bf16[2,32,256]{2,1,0:T(8,128)(2,1)S(1)}, u32[]{:S(2)}, u32[]{:S(2)}) collective-permute-start(bf16[2,32,256]{2,1,0:T(8,128)(2,1)S(1)} %get-tuple-element.27), channel_id=1, source_target_pairs={{0,160},{16,176},{32,128},{48,144},{64,224},{80,240},{96,192},{112... | collective-permute-start | bytes 98312 | tf_op jit(solution)/shard_map/ppermute | solution.py:272
  57.8 0.0 collective-permute-done.8.refs_1_
  57.8 2.8 %collective-permute-start.13 = (bf16[2,32,256]{2,1,0:T(8,128)(2,1)S(1)}, bf16[2,32,256]{2,1,0:T(8,128)(2,1)S(1)}, u32[]{:S(2)}, u32[]{:S(2)}) collective-permute-start(bf16[2,32,256]{2,1,0:T(8,128)(2,1)S(1)} %get-tuple-element.28), channel_id=1, source_target_pairs={{0,192},{16,208},{32,224},{48,240},{64,128},{80,144},{96,160},{112... | collective-permute-start | bytes 98312 | tf_op jit(solution)/shard_map/ppermute | solution.py:272
  60.7 0.0 collective-permute-done.9.refs_2_
  60.7 0.6 collective-permute-start.14
  61.3 0.0 collective-permute-done.10.refs_3_
  61.3 0.0 collective-permute-done.11.refs_4_
  61.3 0.9 %collective-permute-done.12.refs_5_ = bf16[2,32,256]{2,1,0:T(8,128)(2,1)S(1)} collective-permute-done((bf16[2,32,256]{2,1,0:T(8,128)(2,1)S(1)}, bf16[2,32,256]{2,1,0:T(8,128)(2,1)S(1)}, u32[]{:S(2)}, u32[]{:S(2)}) %collective-permute-start.12) | collective-permute-done | bytes 32800 | tf_op jit(solution)/shard_map/ppermute | solution.py:272
  62.2 0.8 collective-permute-done.13.refs_6_
  63.0 0.7 all-to-all-done.x_ref
  63.7 3.4 %row_attention.1 = bf16[16,32,256]{2,1,0:T(8,128)(2,1)} custom-call(bf16[16,32,768]{2,1,0:T(8,128)(2,1)S(1)} %all-to-all-done.x_ref), custom_call_target="tpu_custom_call" | custom-call | flops 536870912 | bytes 1048576 | tf_op jit(solution)/shard_map/row_attention/pallas_call | solution.py:346
  67.0 6.9 %all-to-all-start.1 = ((bf16[16,32,256]{2,1,0:T(8,128)(2,1)}), bf16[16,32,256]{2,1,0:T(8,128)(2,1)S(1)}, u32[]{:S(2)}, u32[]{:S(2)}) async-start(bf16[16,32,256]{2,1,0:T(8,128)(2,1)} %row_attention.1), calls=%async_computation.1 | async-start | bytes 524288 | tf_op jit(solution)/shard_map/all_to_all | solution.py:355
  73.9 0.1 collective-permute-start.15
  74.0 0.9 %fusion = (bf16[256,1024]{1,0:T(8,128)(2,1)S(1)}, bf16[256,1024]{1,0:T(8,128)(2,1)}) fusion(bf16[512,1024]{1,0:T(8,128)(2,1)S(1)} %copy-done.4), kind=kLoop, calls=%fused_computation.15 | loop fusion | bytes 2097152 | tf_op jit(solution)/shard_map/slice | solution.py:381
  74.9 0.5 collective-permute-done.15.cross_ref
  75.4 0.6 copy-done.5
  76.0 4.8 %column_projection.1.acc_ref = f32[512,1024]{1,0:T(8,128)} custom-call(s32[1]{0:T(128)} %bitcast.me_ref, f32[512,1024]{1,0:T(8,128)} %get-tuple-element.18.resid_hbm, bf16[8,32,256]{2,1,0:T(8,128)(2,1)} %copy-done.5, bf16[2,32,256]{2,1,0:T(8,128)(2,1)} %copy-done.3, bf16[2,32,256]{2,1,0:T(8,128)(2,1)} %copy-done.6, bf16[2,32,256]{2,1,0:T(8,128)(2,1)} %copy-done.7, ...), custom_call_target="tpu_custom_call" | custom-call | flops 268435456 | bytes 5242880 | tf_op jit(solution)/shard_map/column_projection/pallas_call | solution.py:360
  80.8 2.1 %all-to-all-done.1.row_ref = bf16[16,32,256]{2,1,0:T(8,128)(2,1)S(1)} async-done(((bf16[16,32,256]{2,1,0:T(8,128)(2,1)}), bf16[16,32,256]{2,1,0:T(8,128)(2,1)S(1)}, u32[]{:S(2)}, u32[]{:S(2)}) %all-to-all-start.1) | async-done | bytes 262176 | tf_op jit(solution)/shard_map/all_to_all | solution.py:355
  83.0 1.6 %copy-done = f32[512,1024]{1,0:T(8,128)S(1)} copy-done((f32[512,1024]{1,0:T(8,128)S(1)}, f32[512,1024]{1,0:T(8,128)}, u32[]{:S(2)}) %copy-start) | copy-done | bytes 2097176
  84.6 1.4 %row_projection.1 = bf16[512,1024]{1,0:T(8,128)(2,1)} custom-call(f32[512,1024]{1,0:T(8,128)S(1)} %copy-done, bf16[16,32,256]{2,1,0:T(8,128)(2,1)S(1)} %all-to-all-done.1.row_ref, bf16[256,1024]{1,0:T(8,128)(2,1)S(1)} %get-tuple-element.31.w_ref), custom_call_target="tpu_custom_call" | custom-call | flops 268435456 | bytes 5242880 | tf_op jit(solution)/shard_map/row_projection/pallas_call | solution.py:374
  (38 shorter events, 0.2 us)
Async XLA Ops:
  0.0 12.0 %copy-start.1 = (bf16[1024,1536]{1,0:T(8,128)(2,1)S(1)}, bf16[1024,1536]{1,0:T(8,128)(2,1)}, u32[]{:S(2)}) copy-start(bf16[1024,1536]{1,0:T(8,128)(2,1)} %w3_hbm.3) | copy-start | bytes 9437188
  12.0 1.2 %copy-start.2 = (bf16[512,1024]{1,0:T(8,128)(2,1)S(1)}, bf16[512,1024]{1,0:T(8,128)(2,1)}, u32[]{:S(2)}) copy-start(bf16[512,1024]{1,0:T(8,128)(2,1)} %get-tuple-element.19.normed_ref) | copy-start | bytes 3145732
  16.0 1.8 %collective-permute-start = (bf16[8,32,768]{2,1,0:T(8,128)(2,1)S(1)}, bf16[8,32,768]{2,1,0:T(8,128)(2,1)S(1)}, u32[]{:S(2)}, u32[]{:S(2)}) collective-permute-start(bf16[8,32,768]{2,1,0:T(8,128)(2,1)S(1)} %get-tuple-element.21), channel_id=1, source_target_pairs={{0,16},{16,0},{32,48},{48,32},{64,80},{80,64},{96,112},{112,96},{1... | collective-permute-start | bytes 1179656 | tf_op jit(solution)/shard_map/ppermute | solution.py:272
  17.9 14.0 %collective-permute-start.1 = (bf16[2,32,768]{2,1,0:T(8,128)(2,1)S(1)}, bf16[2,32,768]{2,1,0:T(8,128)(2,1)S(1)}, u32[]{:S(2)}, u32[]{:S(2)}) collective-permute-start(bf16[2,32,768]{2,1,0:T(8,128)(2,1)S(1)} %pad_maximum_fusion), channel_id=1, source_target_pairs={{0,32},{16,48},{32,0},{48,16},{64,96},{80,112},{96,64},{112,80},{1... | collective-permute-start | bytes 294920 | tf_op jit(solution)/shard_map/ppermute | solution.py:272
  21.2 13.5 %collective-permute-start.2 = (bf16[2,32,768]{2,1,0:T(8,128)(2,1)S(1)}, bf16[2,32,768]{2,1,0:T(8,128)(2,1)S(1)}, u32[]{:S(2)}, u32[]{:S(2)}) collective-permute-start(bf16[2,32,768]{2,1,0:T(8,128)(2,1)S(1)} %pad_maximum_fusion.1), channel_id=1, source_target_pairs={{0,64},{16,80},{32,96},{48,112},{64,0},{80,16},{96,32},{112,48},{1... | collective-permute-start | bytes 294920 | tf_op jit(solution)/shard_map/ppermute | solution.py:272
  22.8 21.8 %collective-permute-start.3 = (bf16[2,32,768]{2,1,0:T(8,128)(2,1)S(1)}, bf16[2,32,768]{2,1,0:T(8,128)(2,1)S(1)}, u32[]{:S(2)}, u32[]{:S(2)}) collective-permute-start(bf16[2,32,768]{2,1,0:T(8,128)(2,1)S(1)} %pad_maximum_fusion.2), channel_id=1, source_target_pairs={{0,96},{16,112},{32,64},{48,80},{64,32},{80,48},{96,0},{112,16},{1... | collective-permute-start | bytes 294920 | tf_op jit(solution)/shard_map/ppermute | solution.py:272
  23.8 20.7 %collective-permute-start.4 = (bf16[2,32,768]{2,1,0:T(8,128)(2,1)}, bf16[2,32,768]{2,1,0:T(8,128)(2,1)S(1)}, u32[]{:S(2)}, u32[]{:S(2)}) collective-permute-start(bf16[2,32,768]{2,1,0:T(8,128)(2,1)} %pad_maximum_fusion.3), channel_id=1, source_target_pairs={{0,128},{16,144},{32,160},{48,176},{64,192},{80,208},{96,224},{112... | collective-permute-start | bytes 294920 | tf_op jit(solution)/shard_map/ppermute | solution.py:272
  27.5 46.5 %copy-start.4 = (bf16[512,1024]{1,0:T(8,128)(2,1)S(1)}, bf16[512,1024]{1,0:T(8,128)(2,1)}, u32[]{:S(2)}) copy-start(bf16[512,1024]{1,0:T(8,128)(2,1)} %param.15) | copy-start | bytes 3145732
  27.5 17.1 %collective-permute-start.5 = (bf16[2,32,768]{2,1,0:T(8,128)(2,1)}, bf16[2,32,768]{2,1,0:T(8,128)(2,1)S(1)}, u32[]{:S(2)}, u32[]{:S(2)}) collective-permute-start(bf16[2,32,768]{2,1,0:T(8,128)(2,1)} %pad_maximum_fusion.4), channel_id=1, source_target_pairs={{0,160},{16,176},{32,128},{48,144},{64,224},{80,240},{96,192},{112... | collective-permute-start | bytes 294920 | tf_op jit(solution)/shard_map/ppermute | solution.py:272
  31.9 12.6 %collective-permute-start.6 = (bf16[2,32,768]{2,1,0:T(8,128)(2,1)}, bf16[2,32,768]{2,1,0:T(8,128)(2,1)S(1)}, u32[]{:S(2)}, u32[]{:S(2)}) collective-permute-start(bf16[2,32,768]{2,1,0:T(8,128)(2,1)} %pad_maximum_fusion.5), channel_id=1, source_target_pairs={{0,192},{16,208},{32,224},{48,240},{64,128},{80,144},{96,160},{112... | collective-permute-start | bytes 294920 | tf_op jit(solution)/shard_map/ppermute | solution.py:272
  34.7 9.9 %collective-permute-start.7 = (bf16[2,32,768]{2,1,0:T(8,128)(2,1)}, bf16[2,32,768]{2,1,0:T(8,128)(2,1)S(1)}, u32[]{:S(2)}, u32[]{:S(2)}) collective-permute-start(bf16[2,32,768]{2,1,0:T(8,128)(2,1)} %pad_maximum_fusion.6), channel_id=1, source_target_pairs={{0,224},{16,240},{32,192},{48,208},{64,160},{80,176},{96,128},{112... | collective-permute-start | bytes 294920 | tf_op jit(solution)/shard_map/ppermute | solution.py:272
  35.0 28.7 %all-to-all-start = ((bf16[16,32,768]{2,1,0:T(8,128)(2,1)}), bf16[16,32,768]{2,1,0:T(8,128)(2,1)S(1)}, u32[]{:S(2)}, u32[]{:S(2)}) async-start(bf16[16,32,768]{2,1,0:T(8,128)(2,1)} %get-tuple-element.30), calls=%async_computation | async-start | bytes 1572864 | tf_op jit(solution)/shard_map/all_to_all | solution.py:317
  46.8 28.5 %copy-start.3 = (bf16[2,32,256]{2,1,0:T(8,128)(2,1)}, bf16[2,32,256]{2,1,0:T(8,128)(2,1)S(1)}, u32[]{:S(2)}) copy-start(bf16[2,32,256]{2,1,0:T(8,128)(2,1)S(1)} %get-tuple-element.22.refs_0_) | copy-start | bytes 98308
  46.8 11.0 %collective-permute-start.8 = (bf16[2,32,256]{2,1,0:T(8,128)(2,1)S(1)}, bf16[2,32,256]{2,1,0:T(8,128)(2,1)S(1)}, u32[]{:S(2)}, u32[]{:S(2)}) collective-permute-start(bf16[2,32,256]{2,1,0:T(8,128)(2,1)S(1)} %get-tuple-element.23), channel_id=1, source_target_pairs={{0,32},{16,48},{32,0},{48,16},{64,96},{80,112},{96,64},{112,80},{1... | collective-permute-start | bytes 98312 | tf_op jit(solution)/shard_map/ppermute | solution.py:272
  49.8 10.8 %collective-permute-start.9 = (bf16[2,32,256]{2,1,0:T(8,128)(2,1)S(1)}, bf16[2,32,256]{2,1,0:T(8,128)(2,1)S(1)}, u32[]{:S(2)}, u32[]{:S(2)}) collective-permute-start(bf16[2,32,256]{2,1,0:T(8,128)(2,1)S(1)} %get-tuple-element.24), channel_id=1, source_target_pairs={{0,64},{16,80},{32,96},{48,112},{64,0},{80,16},{96,32},{112,48},{1... | collective-permute-start | bytes 98312 | tf_op jit(solution)/shard_map/ppermute | solution.py:272
  50.1 11.2 %collective-permute-start.10 = (bf16[2,32,256]{2,1,0:T(8,128)(2,1)S(1)}, bf16[2,32,256]{2,1,0:T(8,128)(2,1)S(1)}, u32[]{:S(2)}, u32[]{:S(2)}) collective-permute-start(bf16[2,32,256]{2,1,0:T(8,128)(2,1)S(1)} %get-tuple-element.25), channel_id=1, source_target_pairs={{0,96},{16,112},{32,64},{48,80},{64,32},{80,48},{96,0},{112,16},{1... | collective-permute-start | bytes 98312 | tf_op jit(solution)/shard_map/ppermute | solution.py:272
  51.9 9.4 %collective-permute-start.11 = (bf16[2,32,256]{2,1,0:T(8,128)(2,1)S(1)}, bf16[2,32,256]{2,1,0:T(8,128)(2,1)S(1)}, u32[]{:S(2)}, u32[]{:S(2)}) collective-permute-start(bf16[2,32,256]{2,1,0:T(8,128)(2,1)S(1)} %get-tuple-element.26), channel_id=1, source_target_pairs={{0,128},{16,144},{32,160},{48,176},{64,192},{80,208},{96,224},{112... | collective-permute-start | bytes 98312 | tf_op jit(solution)/shard_map/ppermute | solution.py:272
  54.1 8.1 %collective-permute-start.12 = (bf16[2,32,256]{2,1,0:T(8,128)(2,1)S(1)}, bf16[2,32,256]{2,1,0:T(8,128)(2,1)S(1)}, u32[]{:S(2)}, u32[]{:S(2)}) collective-permute-start(bf16[2,32,256]{2,1,0:T(8,128)(2,1)S(1)} %get-tuple-element.27), channel_id=1, source_target_pairs={{0,160},{16,176},{32,128},{48,144},{64,224},{80,240},{96,192},{112... | collective-permute-start | bytes 98312 | tf_op jit(solution)/shard_map/ppermute | solution.py:272
  57.8 17.6 %copy-start.6 = (bf16[2,32,256]{2,1,0:T(8,128)(2,1)}, bf16[2,32,256]{2,1,0:T(8,128)(2,1)S(1)}, u32[]{:S(2)}) copy-start(bf16[2,32,256]{2,1,0:T(8,128)(2,1)S(1)} %collective-permute-done.8.refs_1_) | copy-start | bytes 98308
  57.8 5.2 %collective-permute-start.13 = (bf16[2,32,256]{2,1,0:T(8,128)(2,1)S(1)}, bf16[2,32,256]{2,1,0:T(8,128)(2,1)S(1)}, u32[]{:S(2)}, u32[]{:S(2)}) collective-permute-start(bf16[2,32,256]{2,1,0:T(8,128)(2,1)S(1)} %get-tuple-element.28), channel_id=1, source_target_pairs={{0,192},{16,208},{32,224},{48,240},{64,128},{80,144},{96,160},{112... | collective-permute-start | bytes 98312 | tf_op jit(solution)/shard_map/ppermute | solution.py:272
  60.7 14.7 %copy-start.7 = (bf16[2,32,256]{2,1,0:T(8,128)(2,1)}, bf16[2,32,256]{2,1,0:T(8,128)(2,1)S(1)}, u32[]{:S(2)}) copy-start(bf16[2,32,256]{2,1,0:T(8,128)(2,1)S(1)} %collective-permute-done.9.refs_2_) | copy-start | bytes 98308
  60.7 13.3 %collective-permute-start.14 = (bf16[2,32,256]{2,1,0:T(8,128)(2,1)S(1)}, bf16[2,32,256]{2,1,0:T(8,128)(2,1)S(1)}, u32[]{:S(2)}, u32[]{:S(2)}) collective-permute-start(bf16[2,32,256]{2,1,0:T(8,128)(2,1)S(1)} %get-tuple-element.29), channel_id=1, source_target_pairs={{0,224},{16,240},{32,192},{48,208},{64,160},{80,176},{96,128},{112... | collective-permute-start | bytes 98312 | tf_op jit(solution)/shard_map/ppermute | solution.py:272
  61.3 14.1 %copy-start.8 = (bf16[2,32,256]{2,1,0:T(8,128)(2,1)}, bf16[2,32,256]{2,1,0:T(8,128)(2,1)S(1)}, u32[]{:S(2)}) copy-start(bf16[2,32,256]{2,1,0:T(8,128)(2,1)S(1)} %collective-permute-done.10.refs_3_) | copy-start | bytes 98308
  61.3 14.1 %copy-start.9 = (bf16[2,32,256]{2,1,0:T(8,128)(2,1)}, bf16[2,32,256]{2,1,0:T(8,128)(2,1)S(1)}, u32[]{:S(2)}) copy-start(bf16[2,32,256]{2,1,0:T(8,128)(2,1)S(1)} %collective-permute-done.11.refs_4_) | copy-start | bytes 98308
  62.2 13.2 %copy-start.10 = (bf16[2,32,256]{2,1,0:T(8,128)(2,1)}, bf16[2,32,256]{2,1,0:T(8,128)(2,1)S(1)}, u32[]{:S(2)}) copy-start(bf16[2,32,256]{2,1,0:T(8,128)(2,1)S(1)} %collective-permute-done.12.refs_5_) | copy-start | bytes 98308
  63.0 12.4 %copy-start.11 = (bf16[2,32,256]{2,1,0:T(8,128)(2,1)}, bf16[2,32,256]{2,1,0:T(8,128)(2,1)S(1)}, u32[]{:S(2)}) copy-start(bf16[2,32,256]{2,1,0:T(8,128)(2,1)S(1)} %collective-permute-done.13.refs_6_) | copy-start | bytes 98308
  67.0 15.9 %all-to-all-start.1 = ((bf16[16,32,256]{2,1,0:T(8,128)(2,1)}), bf16[16,32,256]{2,1,0:T(8,128)(2,1)S(1)}, u32[]{:S(2)}, u32[]{:S(2)}) async-start(bf16[16,32,256]{2,1,0:T(8,128)(2,1)} %row_attention.1), calls=%async_computation.1 | async-start | bytes 524288 | tf_op jit(solution)/shard_map/all_to_all | solution.py:355
  73.9 1.5 %copy-start.12 = (bf16[2,32,256]{2,1,0:T(8,128)(2,1)}, bf16[2,32,256]{2,1,0:T(8,128)(2,1)S(1)}, u32[]{:S(2)}) copy-start(bf16[2,32,256]{2,1,0:T(8,128)(2,1)S(1)} %collective-permute-done.14.refs_7_) | copy-start | bytes 98308
  73.9 1.4 %collective-permute-start.15 = (bf16[8,32,256]{2,1,0:T(8,128)(2,1)S(1)}, bf16[8,32,256]{2,1,0:T(8,128)(2,1)S(1)}, u32[]{:S(2)}, u32[]{:S(2)}) collective-permute-start(bf16[8,32,256]{2,1,0:T(8,128)(2,1)S(1)} %constant_dynamic-update-slice_fusion), channel_id=1, source_target_pairs={{0,16},{16,0},{32,48},{48,32},{64,80},{80,64},{96,112},{112,96},{1... | collective-permute-start | bytes 393224 | tf_op jit(solution)/shard_map/ppermute | solution.py:272
  75.4 0.7 copy-start.5
  83.0 1.6 %copy-start = (f32[512,1024]{1,0:T(8,128)S(1)}, f32[512,1024]{1,0:T(8,128)}, u32[]{:S(2)}) copy-start(f32[512,1024]{1,0:T(8,128)} %column_projection.1.acc_ref) | copy-start | bytes 6291460

commit v2 on v1

v2 whole, which is shorter than its diff:
```python
import jax
import jax.numpy as jnp
from jax import lax
from jax.experimental import pallas as pl
from jax.experimental.pallas import tpu as pltpu
from jax.sharding import PartitionSpec as P


HD = 64
HB = 8
HR = 4
HC = 4
EPS = 1e-06
NEG = -1e30
LOG2E = 1.4426950408889634
SCALE2 = HD**-0.5 * LOG2E
F32 = jnp.float32
BF16 = jnp.bfloat16

VMEM = pl.BlockSpec(memory_space=pltpu.VMEM)
SMEM = pl.BlockSpec(memory_space=pltpu.SMEM)
HBM = pl.BlockSpec(memory_space=pltpu.HBM)


def dot(a, b):
    return jnp.dot(a, b, preferred_element_type=F32)


def dot_t(a, b):
    return lax.dot_general(a, b, (((1,), (1,)), ((), ())), preferred_element_type=F32)


def halves(pair):
    low = lax.broadcasted_iota(jnp.int32, pair.shape, 1) < HD
    zero = jnp.zeros_like(pair)
    return jnp.concatenate([jnp.where(low, pair, zero), jnp.where(low, zero, pair)], axis=0)


def with_ones(vals2):
    n2 = vals2.shape[0]
    first = lax.broadcasted_iota(jnp.int32, (n2, 2 * HD), 0) < n2 // 2
    low = lax.broadcasted_iota(jnp.int32, (n2, 2 * HD), 1) < HD
    ones = jnp.where(first == low, 1.0, 0.0).astype(BF16)
    return jnp.concatenate([vals2, ones], axis=1)


def pair_attention(query, keys2, vals2, mask):
    n = keys2.shape[0] // 2
    scores = dot_t(query, keys2)
    probs = []
    for h in range(2):
        s = scores[:, h * n : (h + 1) * n]
        if mask is not None:
            s = jnp.where(mask, s, NEG)
        p = jnp.exp2((s - jnp.max(s, axis=-1, keepdims=True)) * SCALE2)
        probs.append(p.astype(BF16))
    mixed = dot(jnp.concatenate(probs, axis=1), vals2)
    return (mixed[:, : 2 * HD] / mixed[:, 2 * HD :]).astype(BF16)


def rms(x, gain):
    scale = lax.rsqrt(jnp.mean(x * x, axis=-1, keepdims=True) + EPS)
    return (x * scale * gain).astype(BF16)


def local_kernel(
    counts_hbm, x_hbm, g1_hbm, g2_hbm, w1_hbm, w2_hbm, w3_hbm, me_ref,
    resid_hbm, row_hbm, *refs,
):
    chips = 8
    cols_hbm = refs[:chips]
    (
        counts, x_ref, g1_ref, g2_ref, w1, w2, w3, normed, qkv, heads,
        resid_ref, row_ref, col_ref, wide, sems, wsems, osems,
    ) = refs[chips:]
    prows, row_flat, _ = row_ref.shape
    tokens, width = resid_ref.shape
    slots = x_hbm.shape[2]
    pcols = x_hbm.shape[1]
    inner = HB * HD
    chip = me_ref[0] // 2
    small = [
        pltpu.make_async_copy(g1_hbm, g1_ref, sems.at[1]),
        pltpu.make_async_copy(g2_hbm, g2_ref, sems.at[2]),
        pltpu.make_async_copy(counts_hbm, counts, sems.at[0]),
    ]
    quarter = prows // 4
    loads = [
        pltpu.make_async_copy(
            x_hbm.at[pl.ds(i * quarter, quarter)], x_ref.at[pl.ds(i * quarter, quarter)], sems.at[3 + i]
        )
        for i in range(4)
    ]
    copies = []
    for i in range(3):
        cols = pl.ds(i * inner, inner)
        copies.append(pltpu.make_async_copy(w1_hbm.at[:, cols], w1.at[:, cols], wsems.at[i]))
    copies.append(pltpu.make_async_copy(w2_hbm, w2, wsems.at[3]))
    for i in range(3):
        cols = pl.ds(i * inner, inner)
        copies.append(pltpu.make_async_copy(w3_hbm.at[:, cols], w3.at[:, cols], wsems.at[4 + i]))
    small[0].start()
    for c in loads + copies[:1] + small[1:] + copies[1:3]:
        c.start()

    small[0].wait()
    g1 = g1_ref[...].astype(F32).reshape(1, width)
    for b in range(tokens // 16):
        if b % (2 * quarter) == 0:
            loads[b // (2 * quarter)].wait()
        normed[pl.ds(b * 16, 16), :] = rms(x_ref[b // pcols, b % pcols].astype(F32), g1)
    for c in copies[3:]:
        c.start()
    for i in range(3):
        copies[i].wait()
        for t in range(inner // 256):
            cols = pl.ds(i * inner + t * 256, 256)
            qkv[:, cols] = dot(normed[...], w1[:, cols]).astype(BF16)

    small[2].wait()
    block = 128
    rowi = lax.broadcasted_iota(jnp.int32, (block, block), 0)
    coli = lax.broadcasted_iota(jnp.int32, (block, block), 1)
    slot = coli % slots
    ngroups = counts.shape[0]
    cap = slots // ngroups
    count = jnp.zeros((block, block), jnp.int32)
    for g in range(ngroups):
        count = jnp.where(slot // cap == g, counts[g], count)
    mask = (rowi // slots == coli // slots) & (slot % cap < count)
    for b in range(tokens // block):
        rows = pl.ds(b * block, block)
        for t in range(HB // 2):
            q = qkv[rows, pl.ds(t * 128, 128)]
            k = qkv[rows, pl.ds(inner + t * 128, 128)]
            v = qkv[rows, pl.ds(2 * inner + t * 128, 128)]
            heads[rows, pl.ds(t * 128, 128)] = pair_attention(q, halves(k), with_ones(halves(v)), mask)

    for c in copies[3:]:
        c.wait()
    small[1].wait()
    g2 = g2_ref[...].astype(F32).reshape(1, width)
    for t in range(width // 256):
        cols = pl.ds(t * 256, 256)
        x = x_ref[:, :, :, cols].reshape(tokens, 256)
        resid_ref[:, cols] = x.astype(F32) + dot(heads[...], w2[:, cols])
    stores = [pltpu.make_async_copy(resid_ref, resid_hbm, osems.at[0])]
    stores[0].start()
    for b in range(tokens // 16):
        rows = pl.ds(b * 16, 16)
        normed[rows, :] = rms(resid_ref[rows, :], g2)

    for i in range(3):
        to = pl.ds(i * 256, 256)
        w = dot(normed[...], w3[:, pl.ds(i * inner + 256, 256)])
        wide[i % 2, 0] = w[:, :128]
        wide[i % 2, 1] = w[:, 128:]
        for d in range(chips):
            for low in range(2):
                s = 2 * (chip ^ d) + low
                for c in range(pcols):
                    part = [
                        wide[i % 2, j, pl.ds(c * slots + s, prows, stride=pcols * slots), :]
                        for j in range(2)
                    ]
                    at = pl.ds((low * pcols + c) * prows, prows)
                    col_ref[d, at, to] = jnp.concatenate(part, axis=1).astype(BF16)
    for d in range(chips):
        stores.append(pltpu.make_async_copy(col_ref.at[d], cols_hbm[d], osems.at[1 + d]))
        stores[-1].start()
    for i in range(3):
        to = pl.ds(i * 256, 256)
        r = dot(normed[...], w3[:, pl.ds(i * inner, 256)]).astype(BF16)
        row_ref[:, :, to] = r.reshape(prows, row_flat, 256)
        stores.append(
            pltpu.make_async_copy(row_ref.at[:, :, to], row_hbm.at[:, :, to], osems.at[1 + chips + i])
        )
        stores[-1].start()
    for c in stores:
        c.wait()


def row_kernel(x_ref, o_ref, flat):
    n, each, _ = x_ref.shape
    slots = 16
    m = n * each
    block = 128
    rowi = lax.broadcasted_iota(jnp.int32, (block, m), 0)
    coli = lax.broadcasted_iota(jnp.int32, (block, m), 1)
    mask = rowi % slots == coli % slots
    x = x_ref[...].reshape(m, 3 * HR * HD)
    for t in range(HR // 2):
        k = halves(x[:, 256 + t * 128 : 384 + t * 128])
        v = with_ones(halves(x[:, 512 + t * 128 : 640 + t * 128]))
        for b in range(m // block):
            q = x[b * block : (b + 1) * block, t * 128 : (t + 1) * 128]
            flat[pl.ds(b * block, block), pl.ds(t * 128, 128)] = pair_attention(q, k, v, mask)
    o_ref[...] = flat[...].reshape(n, each, HR * HD)


def col_kernel(own_ref, cross_ref, *refs):
    n = len(refs) // 2
    pieces, outs = (own_ref,) + refs[:n], refs[n:]
    prows = 16
    each = cross_ref.shape[1]
    others = [cross_ref.at[d] for d in range(len(pieces))]
    for g in range(each // prows):
        part = pl.ds(g * prows, prows)

        def take(refs_, at):
            return jnp.concatenate([r[part, pl.ds(at, 128)] for r in refs_], axis=0)

        for t in range(HC // 2):
            at = t * 128
            k = halves(jnp.concatenate([take(pieces, 256 + at), take(others, at)], axis=0))
            v = with_ones(halves(jnp.concatenate([take(pieces, 512 + at), take(others, 256 + at)], axis=0)))
            o = pair_attention(take(pieces, at), k, v, None)
            for d in range(len(pieces)):
                outs[d][part, pl.ds(at, 128)] = o[d * prows : (d + 1) * prows]


def mid_kernel(me_ref, resid_hbm, *refs):
    pieces, (w_ref, acc_ref, wide, natural, resid_ref, rsems) = refs[:8], refs[8:]
    loads = []
    for t in range(acc_ref.shape[1] // 256):
        cols = pl.ds(t * 256, 256)
        loads.append(pltpu.make_async_copy(resid_hbm.at[:, cols], resid_ref.at[:, cols], rsems.at[t]))
        loads[t].start()
    slots = 2 * len(pieces)
    each = pieces[0].shape[0]
    prows = 16
    pcols = each // 2 // prows
    chip = me_ref[0] // 2
    for d in range(len(pieces)):
        to = pl.ds(pl.multiple_of((chip ^ d) * each, each), each)
        for j in range(2):
            wide[j, to, :] = pieces[d][:, pl.ds(j * 128, 128)].astype(F32)
    for r in range(prows):
        for c in range(pcols):
            part = [
                wide[j, pl.ds(c * prows + r, slots, stride=pcols * prows), :] for j in range(2)
            ]
            natural[pl.ds((r * pcols + c) * slots, slots), :] = jnp.concatenate(part, axis=1).astype(BF16)
    for t in range(acc_ref.shape[1] // 256):
        cols = pl.ds(t * 256, 256)
        loads[t].wait()
        acc_ref[:, cols] = resid_ref[:, cols] + dot(natural[...], w_ref[:, cols])


def last_kernel(acc_ref, row_ref, w_ref, out_ref):
    m = acc_ref.shape[0]
    heads = row_ref[...].reshape(m, row_ref.shape[2])
    for t in range(acc_ref.shape[1] // 256):
        cols = pl.ds(t * 256, 256)
        out_ref[:, cols] = (acc_ref[:, cols] + dot(heads, w_ref[:, cols])).astype(BF16)


def cost(flops, nbytes, trans=0):
    return pl.CostEstimate(flops=flops, bytes_accessed=nbytes, transcendentals=trans)


def flip(array, axes, n, by):
    return lax.ppermute(array, axes, [(i, i ^ by) for i in range(n)])


def local(tokens, counts, norm_band, w_band_qkv, w_band_out, norm_space, w_space_qkv, w_space_out):
    prows, pcols, slots, width = tokens.shape
    m = prows * pcols * slots
    inner = HB * HD
    wide = 3 * HR * HD
    half = slots // 2
    each = 2 * pcols * prows
    rows_axes = ("band", "row")
    me = lax.axis_index(rows_axes).astype(jnp.int32).reshape(1)

    def params(mib):
        return pltpu.CompilerParams(vmem_limit_bytes=mib << 20)

    resid, row_qkv, *col_qkv = pl.pallas_call(
        local_kernel,
        name="local",
        out_shape=(jax.ShapeDtypeStruct((m, width), F32), jax.ShapeDtypeStruct((prows, pcols * slots, wide), BF16))
        + (jax.ShapeDtypeStruct((each, wide), BF16),) * half,
        in_specs=[HBM] * 7 + [SMEM],
        out_specs=(HBM,) * (2 + half),
        scratch_shapes=[
            pltpu.SMEM(counts.shape, jnp.int32),
            pltpu.VMEM(tokens.shape, BF16),
            pltpu.VMEM((width,), BF16),
            pltpu.VMEM((width,), BF16),
            pltpu.VMEM(w_band_qkv.shape, BF16),
            pltpu.VMEM(w_band_out.shape, BF16),
            pltpu.VMEM(w_space_qkv.shape, BF16),
            pltpu.VMEM((m, width), BF16),
            pltpu.VMEM((m, 3 * inner), BF16),
            pltpu.VMEM((m, inner), BF16),
            pltpu.VMEM((m, width), F32),
            pltpu.VMEM((prows, pcols * slots, wide), BF16),
            pltpu.VMEM((half, each, wide), BF16),
            pltpu.VMEM((2, 2, m, 128), F32),
            pltpu.SemaphoreType.DMA((7,)),
            pltpu.SemaphoreType.DMA((7,)),
            pltpu.SemaphoreType.DMA((4 + half,)),
        ],
        compiler_params=params(59),
        cost_estimate=cost(2 * m * width * 4096, 12 << 20),
    )(counts, tokens, norm_band, norm_space, w_band_qkv, w_band_out, w_space_qkv, me)
    row_all = lax.all_to_all(row_qkv, "col", 0, 0, tiled=True)
    got = []
    for d in range(1, half):
        got.append(flip(col_qkv[d], rows_axes, slots, 2 * d))
    pack = jnp.stack([g[:, HC * HD :] for g in [col_qkv[0]] + got])
    cross = flip(pack, rows_axes, slots, 1)
    row_o = pl.pallas_call(
        row_kernel,
        name="row_attention",
        out_shape=jax.ShapeDtypeStruct((prows, pcols * slots, HR * HD), BF16),
        in_specs=[VMEM], out_specs=VMEM,
        scratch_shapes=[pltpu.VMEM((m, HR * HD), BF16)],
        compiler_params=params(16),
        cost_estimate=cost(1 << 29, 1 << 20),
    )(row_all)
    row_heads = lax.all_to_all(row_o, "col", 0, 0, tiled=True)
    col_o = pl.pallas_call(
        col_kernel,
        name="column_attention",
        out_shape=(jax.ShapeDtypeStruct((each, HC * HD), BF16),) * half,
        in_specs=[VMEM] * (half + 1),
        out_specs=(VMEM,) * half,
        compiler_params=params(16),
        cost_estimate=cost(1 << 28, 1 << 20),
    )(col_qkv[0], cross, *got)
    back = [col_o[0]]
    for d in range(1, half):
        back.append(flip(col_o[d], rows_axes, slots, 2 * d))
    acc = pl.pallas_call(
        mid_kernel,
        name="column_projection",
        out_shape=jax.ShapeDtypeStruct((m, width), F32),
        in_specs=[SMEM, HBM] + [VMEM] * half + [VMEM], out_specs=VMEM,
        scratch_shapes=[
            pltpu.VMEM((2, m, 128), F32),
            pltpu.VMEM((m, HC * HD), BF16),
            pltpu.VMEM((m, width), F32),
            pltpu.SemaphoreType.DMA((width // 256,)),
        ],
        compiler_params=params(16),
        cost_estimate=cost(2 * m * width * 256, 5 << 20),
    )(me, resid, *back, w_space_out[HR * HD :])
    out = pl.pallas_call(
        last_kernel,
        name="row_projection",
        out_shape=jax.ShapeDtypeStruct((m, width), BF16),
        in_specs=[VMEM, VMEM, VMEM], out_specs=VMEM,
        compiler_params=params(16),
        cost_estimate=cost(2 * m * width * 256, 5 << 20),
    )(acc, row_heads, w_space_out[: HR * HD])
    return out.reshape(prows, pcols, slots, width)


def solution(mesh):
    placed = (P(("band", "row"), "col", None, None), P(), P(), P(), P(), P(), P(), P())
    return jax.shard_map(
        local,
        mesh=mesh,
        in_specs=placed,
        out_specs=P(("band", "row"), "col", None, None),
        check_vma=False,
    )
```

time: 86.3 us -> 81.4 us (0.943)
  Pallas kernels: 26.6 us -> 15.6 us
  starting transfers between devices: 45.5 us -> 51.9 us
  local copies, waits for them, and re-layouts: 4.38 us -> 7.54 us
  other arithmetic: 2.62 us -> 0 us
  waiting for transfers between devices: 6.63 us -> 5.54 us
    ppermute x16 -> x15, starting transfers between devices: 29 us -> 34.6 us  [flip(): return lax.ppermute(array, axes, [(i, i ^ by) for i in range(n)])]
    unnamed x33 -> x13, local copies, waits for them, and re-layouts: 3.46 us -> 6.85 us
    pallas_call x1, Pallas kernels: 12 us -> 8.91 us  [local(): pl.pallas_call(local_kernel, name='local', out_shape=(jax.ShapeDtypeStruc...]
    pallas_call x1 -> x0, Pallas kernels: 2.83 us -> none  [local(): pl.pallas_call(column_qkv_kernel, name='column_qkv', out_shape=(jax.Shape...]
    pallas_call x1, Pallas kernels: 4.8 us -> 2.03 us  [local(): pl.pallas_call(mid_kernel, name='column_projection', out_shape=jax.ShapeD...]
    another operation x7 -> x0, other arithmetic: 2.62 us -> none  [local(): got.append(flip(jnp.stack([keep[d], cross[d]]), rows_axes, slots, 2 * d))]
    all_to_all x1, waiting for transfers between devices: 2.12 us -> 0.01 us  [local(): row_heads = lax.all_to_all(row_o, 'col', 0, 0, tiled=True)]
    ppermute x16 -> x15, waiting for transfers between devices: 3.85 us -> 5.53 us  [flip(): return lax.ppermute(array, axes, [(i, i ^ by) for i in range(n)])]
  transfers between devices with their start and end apart: 18 -> 17, of which waited for: 6 -> 4; matrix products, arithmetic and copies ran while one was open for 4% -> 7% of each run, Pallas kernels for 12% -> 7%
where the time goes in v2:
time: 81.4 us; the launch traced here: 80.7 us
  starting transfers between devices  51.9 us (64%)
  Pallas kernels  15.6 us (19%)
  local copies, waits for them, and re-layouts  7.54 us (9%)
  waiting for transfers between devices  5.54 us (7%)
    ppermute x15, starting transfers between devices, flip(): return lax.ppermute(array, axes, [(i, i ^ by) for i in range(n)])  34.6 us
    all_to_all x1, starting transfers between devices, local(): row_all = lax.all_to_all(row_qkv, 'col', 0, 0, tiled=True)  9.74 us
    pallas_call x1, Pallas kernels, local(): pl.pallas_call(local_kernel, name='local', out_shape=(jax.ShapeDtypeStruc...  8.91 us
    all_to_all x1, starting transfers between devices, local(): row_heads = lax.all_to_all(row_o, 'col', 0, 0, tiled=True)  7.52 us
    unnamed x13, local copies, waits for them, and re-layouts  6.85 us
    ppermute x15, waiting for transfers between devices, flip(): return lax.ppermute(array, axes, [(i, i ^ by) for i in range(n)])  5.53 us
    pallas_call x1, Pallas kernels, local(): pl.pallas_call(row_kernel, name='row_attention', out_shape=jax.ShapeDtype...  2.32 us
    pallas_call x1, Pallas kernels, local(): pl.pallas_call(mid_kernel, name='column_projection', out_shape=jax.ShapeD...  2.03 us
  transfers between devices with their start and end apart: 17, of which 4 were waited for; matrix products, arithmetic and copies ran while one was open for 7% of the time, Pallas kernels for 7%

profile of v2, /device:TPU:32, one launch (start us, length us, event | category | flops | bytes accessed | tf_op | source)
XLA Modules:
  0.0 80.7 jit_solution(8820150707977862893)
XLA Ops:
  0.0 8.9 %local.1 = (f32[512,1024]{1,0:T(8,128)}, bf16[16,32,768]{2,1,0:T(8,128)(2,1)}, bf16[64,768]{1,0:T(8,128)(2,1)}, bf16[64,768]{1,0:T(8,128)(2,1)}, bf16[64,768]{1,...) custom-call(s32[4]{0:T(128)} %counts_hbm.1, ...), custom_call_target="tpu_custom_call" | custom-call | flops 4294967296 | bytes 12582912 | tf_op jit(solution)/shard_map/local/pallas_call | solution.py:279
  8.9 0.0 copy-start.2
  8.9 9.7 %all-to-all-start = ((bf16[16,32,768]{2,1,0:T(8,128)(2,1)}), bf16[16,32,768]{2,1,0:T(8,128)(2,1)S(1)}, u32[]{:S(2)}, u32[]{:S(2)}) async-start(bf16[16,32,768]{2,1,0:T(8,128)(2,1)} %get-tuple-element.40), calls=%async_computation | async-start | bytes 1572864 | tf_op jit(solution)/shard_map/all_to_all | solution.py:308
  18.7 2.9 %collective-permute-start = (bf16[64,768]{1,0:T(8,128)(2,1)}, bf16[64,768]{1,0:T(8,128)(2,1)S(1)}, u32[]{:S(2)}, u32[]{:S(2)}) collective-permute-start(bf16[64,768]{1,0:T(8,128)(2,1)} %get-tuple-element.25), channel_id=1, source_target_pairs={{0,32},{16,48},{32,0},{48,16},{64,96},{80,112},{96,64},{112,80},{1... | collective-permute-start | bytes 294920 | tf_op jit(solution)/shard_map/ppermute | solution.py:263
  21.6 1.5 %collective-permute-start.1 = (bf16[64,768]{1,0:T(8,128)(2,1)}, bf16[64,768]{1,0:T(8,128)(2,1)S(1)}, u32[]{:S(2)}, u32[]{:S(2)}) collective-permute-start(bf16[64,768]{1,0:T(8,128)(2,1)} %get-tuple-element.26), channel_id=1, source_target_pairs={{0,64},{16,80},{32,96},{48,112},{64,0},{80,16},{96,32},{112,48},{1... | collective-permute-start | bytes 294920 | tf_op jit(solution)/shard_map/ppermute | solution.py:263
  23.1 0.6 collective-permute-start.2
  23.7 3.0 %collective-permute-start.3 = (bf16[64,768]{1,0:T(8,128)(2,1)}, bf16[64,768]{1,0:T(8,128)(2,1)S(1)}, u32[]{:S(2)}, u32[]{:S(2)}) collective-permute-start(bf16[64,768]{1,0:T(8,128)(2,1)} %get-tuple-element.28), channel_id=1, source_target_pairs={{0,128},{16,144},{32,160},{48,176},{64,192},{80,208},{96,224},{112... | collective-permute-start | bytes 294920 | tf_op jit(solution)/shard_map/ppermute | solution.py:263
  26.7 2.8 %collective-permute-start.4 = (bf16[64,768]{1,0:T(8,128)(2,1)}, bf16[64,768]{1,0:T(8,128)(2,1)S(1)}, u32[]{:S(2)}, u32[]{:S(2)}) collective-permute-start(bf16[64,768]{1,0:T(8,128)(2,1)} %get-tuple-element.29), channel_id=1, source_target_pairs={{0,160},{16,176},{32,128},{48,144},{64,224},{80,240},{96,192},{112... | collective-permute-start | bytes 294920 | tf_op jit(solution)/shard_map/ppermute | solution.py:263
  29.6 1.5 %bitcast_dynamic-update-slice_fusion = bf16[8,64,512]{2,1,0:T(8,128)(2,1)} fusion(bf16[64,768]{1,0:T(8,128)(2,1)} %get-tuple-element.24.own_ref), kind=kLoop, calls=%fused_computation.14 | loop fusion | bytes 131072
  31.0 0.0 collective-permute-done.refs_0_
  31.0 2.8 %collective-permute-start.5 = (bf16[64,768]{1,0:T(8,128)(2,1)}, bf16[64,768]{1,0:T(8,128)(2,1)S(1)}, u32[]{:S(2)}, u32[]{:S(2)}) collective-permute-start(bf16[64,768]{1,0:T(8,128)(2,1)} %get-tuple-element.30), channel_id=1, source_target_pairs={{0,192},{16,208},{32,224},{48,240},{64,128},{80,144},{96,160},{112... | collective-permute-start | bytes 294920 | tf_op jit(solution)/shard_map/ppermute | solution.py:263
  33.8 0.6 fusion.6
  34.5 0.0 collective-permute-done.1.refs_1_
  34.5 3.4 %collective-permute-start.6 = (bf16[64,768]{1,0:T(8,128)(2,1)}, bf16[64,768]{1,0:T(8,128)(2,1)S(1)}, u32[]{:S(2)}, u32[]{:S(2)}) collective-permute-start(bf16[64,768]{1,0:T(8,128)(2,1)} %get-tuple-element.31), channel_id=1, source_target_pairs={{0,224},{16,240},{32,192},{48,208},{64,160},{80,176},{96,128},{112... | collective-permute-start | bytes 294920 | tf_op jit(solution)/shard_map/ppermute | solution.py:263
  37.8 0.6 fusion.5
  38.5 0.0 collective-permute-done.2.refs_2_
  38.5 0.6 fusion.4
  39.1 0.0 collective-permute-done.3.refs_3_
  39.1 0.6 fusion.3
  39.7 0.0 collective-permute-done.4.refs_4_
  39.7 0.6 fusion.2
  40.4 0.0 collective-permute-done.5.refs_5_
  40.4 0.6 fusion.1
  41.0 1.9 %collective-permute-done.6.refs_6_ = bf16[64,768]{1,0:T(8,128)(2,1)S(1)} collective-permute-done((bf16[64,768]{1,0:T(8,128)(2,1)}, bf16[64,768]{1,0:T(8,128)(2,1)S(1)}, u32[]{:S(2)}, u32[]{:S(2)}) %collective-permute-start.6) | collective-permute-done | bytes 98336 | tf_op jit(solution)/shard_map/ppermute | solution.py:263
  42.9 0.6 fusion
  43.5 0.0 collective-permute-start.7
  43.5 0.0 all-to-all-done.x_ref
  43.5 2.3 %row_attention.1 = bf16[16,32,256]{2,1,0:T(8,128)(2,1)} custom-call(bf16[16,32,768]{2,1,0:T(8,128)(2,1)S(1)} %all-to-all-done.x_ref), custom_call_target="tpu_custom_call" | custom-call | flops 536870912 | bytes 1048576 | tf_op jit(solution)/shard_map/row_attention/pallas_call | solution.py:314
  45.8 7.5 %all-to-all-start.1 = ((bf16[16,32,256]{2,1,0:T(8,128)(2,1)}), bf16[16,32,256]{2,1,0:T(8,128)(2,1)S(1)}, u32[]{:S(2)}, u32[]{:S(2)}) async-start(bf16[16,32,256]{2,1,0:T(8,128)(2,1)} %row_attention.1), calls=%async_computation.1 | async-start | bytes 524288 | tf_op jit(solution)/shard_map/all_to_all | solution.py:323
  53.4 0.0 collective-permute-done.7.cross_ref
  53.4 0.9 %column_attention.1 = (bf16[64,256]{1,0:T(8,128)(2,1)S(1)}, bf16[64,256]{1,0:T(8,128)(2,1)S(1)}, bf16[64,256]{1,0:T(8,128)(2,1)S(1)}, bf16[64,256]{1,0:T(8,128)(...) custom-call(bf16[64,768]{1,0:T(8,128)(2,1)S(1)} %copy-done.1, ...), custom_call_target="tpu_custom_call" | custom-call | flops 268435456 | bytes 1048576 | tf_op jit(solution)/shard_map/column_attention/pallas_call | solution.py:324
  54.3 5.5 %collective-permute-start.8 = (bf16[64,256]{1,0:T(8,128)(2,1)S(1)}, bf16[64,256]{1,0:T(8,128)(2,1)S(1)}, u32[]{:S(2)}, u32[]{:S(2)}) collective-permute-start(bf16[64,256]{1,0:T(8,128)(2,1)S(1)} %get-tuple-element.33), channel_id=1, source_target_pairs={{0,32},{16,48},{32,0},{48,16},{64,96},{80,112},{96,64},{112,80},{1... | collective-permute-start | bytes 98312 | tf_op jit(solution)/shard_map/ppermute | solution.py:263
  59.9 1.1 %collective-permute-start.9 = (bf16[64,256]{1,0:T(8,128)(2,1)S(1)}, bf16[64,256]{1,0:T(8,128)(2,1)S(1)}, u32[]{:S(2)}, u32[]{:S(2)}) collective-permute-start(bf16[64,256]{1,0:T(8,128)(2,1)S(1)} %get-tuple-element.34), channel_id=1, source_target_pairs={{0,64},{16,80},{32,96},{48,112},{64,0},{80,16},{96,32},{112,48},{1... | collective-permute-start | bytes 98312 | tf_op jit(solution)/shard_map/ppermute | solution.py:263
  61.0 1.8 %collective-permute-start.10 = (bf16[64,256]{1,0:T(8,128)(2,1)S(1)}, bf16[64,256]{1,0:T(8,128)(2,1)S(1)}, u32[]{:S(2)}, u32[]{:S(2)}) collective-permute-start(bf16[64,256]{1,0:T(8,128)(2,1)S(1)} %get-tuple-element.35), channel_id=1, source_target_pairs={{0,96},{16,112},{32,64},{48,80},{64,32},{80,48},{96,0},{112,16},{1... | collective-permute-start | bytes 98312 | tf_op jit(solution)/shard_map/ppermute | solution.py:263
  62.7 2.1 %collective-permute-start.11 = (bf16[64,256]{1,0:T(8,128)(2,1)S(1)}, bf16[64,256]{1,0:T(8,128)(2,1)S(1)}, u32[]{:S(2)}, u32[]{:S(2)}) collective-permute-start(bf16[64,256]{1,0:T(8,128)(2,1)S(1)} %get-tuple-element.36), channel_id=1, source_target_pairs={{0,128},{16,144},{32,160},{48,176},{64,192},{80,208},{96,224},{112... | collective-permute-start | bytes 98312 | tf_op jit(solution)/shard_map/ppermute | solution.py:263
  64.8 3.0 %collective-permute-start.12 = (bf16[64,256]{1,0:T(8,128)(2,1)S(1)}, bf16[64,256]{1,0:T(8,128)(2,1)S(1)}, u32[]{:S(2)}, u32[]{:S(2)}) collective-permute-start(bf16[64,256]{1,0:T(8,128)(2,1)S(1)} %get-tuple-element.37), channel_id=1, source_target_pairs={{0,160},{16,176},{32,128},{48,144},{64,224},{80,240},{96,192},{112... | collective-permute-start | bytes 98312 | tf_op jit(solution)/shard_map/ppermute | solution.py:263
  67.8 0.3 collective-permute-start.13
  68.1 0.0 collective-permute-done.9.refs_2_
  68.1 3.8 %collective-permute-start.14 = (bf16[64,256]{1,0:T(8,128)(2,1)S(1)}, bf16[64,256]{1,0:T(8,128)(2,1)S(1)}, u32[]{:S(2)}, u32[]{:S(2)}) collective-permute-start(bf16[64,256]{1,0:T(8,128)(2,1)S(1)} %get-tuple-element.39), channel_id=1, source_target_pairs={{0,224},{16,240},{32,192},{48,208},{64,160},{80,176},{96,128},{112... | collective-permute-start | bytes 98312 | tf_op jit(solution)/shard_map/ppermute | solution.py:263
  71.9 0.1 fusion.7
  72.0 0.0 collective-permute-done.10.refs_3_
  72.0 0.6 collective-permute-done.12.refs_5_
  72.6 0.3 collective-permute-done.13.refs_6_
  72.9 2.7 %collective-permute-done.14.refs_7_ = bf16[64,256]{1,0:T(8,128)(2,1)S(1)} collective-permute-done((bf16[64,256]{1,0:T(8,128)(2,1)S(1)}, bf16[64,256]{1,0:T(8,128)(2,1)S(1)}, u32[]{:S(2)}, u32[]{:S(2)}) %collective-permute-start.14) | collective-permute-done | bytes 32800 | tf_op jit(solution)/shard_map/ppermute | solution.py:263
  75.6 1.6 %copy-done = f32[512,1024]{1,0:T(8,128)S(1)} copy-done((f32[512,1024]{1,0:T(8,128)S(1)}, f32[512,1024]{1,0:T(8,128)}, u32[]{:S(2)}) %copy-start) | copy-done | bytes 2097176
  77.2 2.0 %column_projection.1.acc_ref = f32[512,1024]{1,0:T(8,128)S(1)} custom-call(s32[1]{0:T(128)} %bitcast.me_ref, f32[512,1024]{1,0:T(8,128)S(1)} %copy-done, bf16[64,256]{1,0:T(8,128)(2,1)S(1)} %get-tuple-element.32.refs_0_, bf16[64,256]{1,0:T(8,128)(2,1)S(1)} %collective-permute-done.8.refs_1_, bf16[64,256]{1,0:T(8,128)(2,1)S(1)} %collective-permute-done.9.refs_2_, ...), custom_call_target="tpu_custom_call" | custom-call | flops 268435456 | bytes 5242880 | tf_op jit(solution)/shard_map/column_projection/pallas_call | solution.py:336
  79.3 0.0 all-to-all-done.1.row_ref
  79.3 1.4 %row_projection.1 = bf16[512,1024]{1,0:T(8,128)(2,1)} custom-call(f32[512,1024]{1,0:T(8,128)S(1)} %column_projection.1.acc_ref, bf16[16,32,256]{2,1,0:T(8,128)(2,1)S(1)} %all-to-all-done.1.row_ref, bf16[256,1024]{1,0:T(8,128)(2,1)S(1)} %get-tuple-element.41.w_ref), custom_call_target="tpu_custom_call" | custom-call | flops 268435456 | bytes 5242880 | tf_op jit(solution)/shard_map/row_projection/pallas_call | solution.py:350
  (6 shorter events, 0.0 us)
Async XLA Ops:
  8.9 44.5 %copy-start.1 = (bf16[64,768]{1,0:T(8,128)(2,1)S(1)}, bf16[64,768]{1,0:T(8,128)(2,1)}, u32[]{:S(2)}) copy-start(bf16[64,768]{1,0:T(8,128)(2,1)} %get-tuple-element.24.own_ref) | copy-start | bytes 294916
  8.9 63.0 %copy-start.2 = (bf16[512,1024]{1,0:T(8,128)(2,1)S(1)}, bf16[512,1024]{1,0:T(8,128)(2,1)}, u32[]{:S(2)}) copy-start(bf16[512,1024]{1,0:T(8,128)(2,1)} %param.15) | copy-start | bytes 3145732
  8.9 34.6 %all-to-all-start = ((bf16[16,32,768]{2,1,0:T(8,128)(2,1)}), bf16[16,32,768]{2,1,0:T(8,128)(2,1)S(1)}, u32[]{:S(2)}, u32[]{:S(2)}) async-start(bf16[16,32,768]{2,1,0:T(8,128)(2,1)} %get-tuple-element.40), calls=%async_computation | async-start | bytes 1572864 | tf_op jit(solution)/shard_map/all_to_all | solution.py:308
  18.7 12.3 %collective-permute-start = (bf16[64,768]{1,0:T(8,128)(2,1)}, bf16[64,768]{1,0:T(8,128)(2,1)S(1)}, u32[]{:S(2)}, u32[]{:S(2)}) collective-permute-start(bf16[64,768]{1,0:T(8,128)(2,1)} %get-tuple-element.25), channel_id=1, source_target_pairs={{0,32},{16,48},{32,0},{48,16},{64,96},{80,112},{96,64},{112,80},{1... | collective-permute-start | bytes 294920 | tf_op jit(solution)/shard_map/ppermute | solution.py:263
  21.6 12.9 %collective-permute-start.1 = (bf16[64,768]{1,0:T(8,128)(2,1)}, bf16[64,768]{1,0:T(8,128)(2,1)S(1)}, u32[]{:S(2)}, u32[]{:S(2)}) collective-permute-start(bf16[64,768]{1,0:T(8,128)(2,1)} %get-tuple-element.26), channel_id=1, source_target_pairs={{0,64},{16,80},{32,96},{48,112},{64,0},{80,16},{96,32},{112,48},{1... | collective-permute-start | bytes 294920 | tf_op jit(solution)/shard_map/ppermute | solution.py:263
  23.1 15.4 %collective-permute-start.2 = (bf16[64,768]{1,0:T(8,128)(2,1)}, bf16[64,768]{1,0:T(8,128)(2,1)S(1)}, u32[]{:S(2)}, u32[]{:S(2)}) collective-permute-start(bf16[64,768]{1,0:T(8,128)(2,1)} %get-tuple-element.27), channel_id=1, source_target_pairs={{0,96},{16,112},{32,64},{48,80},{64,32},{80,48},{96,0},{112,16},{1... | collective-permute-start | bytes 294920 | tf_op jit(solution)/shard_map/ppermute | solution.py:263
  23.7 15.4 %collective-permute-start.3 = (bf16[64,768]{1,0:T(8,128)(2,1)}, bf16[64,768]{1,0:T(8,128)(2,1)S(1)}, u32[]{:S(2)}, u32[]{:S(2)}) collective-permute-start(bf16[64,768]{1,0:T(8,128)(2,1)} %get-tuple-element.28), channel_id=1, source_target_pairs={{0,128},{16,144},{32,160},{48,176},{64,192},{80,208},{96,224},{112... | collective-permute-start | bytes 294920 | tf_op jit(solution)/shard_map/ppermute | solution.py:263
  26.7 13.0 %collective-permute-start.4 = (bf16[64,768]{1,0:T(8,128)(2,1)}, bf16[64,768]{1,0:T(8,128)(2,1)S(1)}, u32[]{:S(2)}, u32[]{:S(2)}) collective-permute-start(bf16[64,768]{1,0:T(8,128)(2,1)} %get-tuple-element.29), channel_id=1, source_target_pairs={{0,160},{16,176},{32,128},{48,144},{64,224},{80,240},{96,192},{112... | collective-permute-start | bytes 294920 | tf_op jit(solution)/shard_map/ppermute | solution.py:263
  31.0 9.4 %collective-permute-start.5 = (bf16[64,768]{1,0:T(8,128)(2,1)}, bf16[64,768]{1,0:T(8,128)(2,1)S(1)}, u32[]{:S(2)}, u32[]{:S(2)}) collective-permute-start(bf16[64,768]{1,0:T(8,128)(2,1)} %get-tuple-element.30), channel_id=1, source_target_pairs={{0,192},{16,208},{32,224},{48,240},{64,128},{80,144},{96,160},{112... | collective-permute-start | bytes 294920 | tf_op jit(solution)/shard_map/ppermute | solution.py:263
  34.5 8.4 %collective-permute-start.6 = (bf16[64,768]{1,0:T(8,128)(2,1)}, bf16[64,768]{1,0:T(8,128)(2,1)S(1)}, u32[]{:S(2)}, u32[]{:S(2)}) collective-permute-start(bf16[64,768]{1,0:T(8,128)(2,1)} %get-tuple-element.31), channel_id=1, source_target_pairs={{0,224},{16,240},{32,192},{48,208},{64,160},{80,176},{96,128},{112... | collective-permute-start | bytes 294920 | tf_op jit(solution)/shard_map/ppermute | solution.py:263
  43.5 9.9 %collective-permute-start.7 = (bf16[8,64,512]{2,1,0:T(8,128)(2,1)}, bf16[8,64,512]{2,1,0:T(8,128)(2,1)S(1)}, u32[]{:S(2)}, u32[]{:S(2)}) collective-permute-start(bf16[8,64,512]{2,1,0:T(8,128)(2,1)} %fusion), channel_id=1, source_target_pairs={{0,16},{16,0},{32,48},{48,32},{64,80},{80,64},{96,112},{112,96},{1... | collective-permute-start | bytes 1572872 | tf_op jit(solution)/shard_map/ppermute | solution.py:263
  45.8 33.4 %all-to-all-start.1 = ((bf16[16,32,256]{2,1,0:T(8,128)(2,1)}), bf16[16,32,256]{2,1,0:T(8,128)(2,1)S(1)}, u32[]{:S(2)}, u32[]{:S(2)}) async-start(bf16[16,32,256]{2,1,0:T(8,128)(2,1)} %row_attention.1), calls=%async_computation.1 | async-start | bytes 524288 | tf_op jit(solution)/shard_map/all_to_all | solution.py:323
  54.3 13.5 %collective-permute-start.8 = (bf16[64,256]{1,0:T(8,128)(2,1)S(1)}, bf16[64,256]{1,0:T(8,128)(2,1)S(1)}, u32[]{:S(2)}, u32[]{:S(2)}) collective-permute-start(bf16[64,256]{1,0:T(8,128)(2,1)S(1)} %get-tuple-element.33), channel_id=1, source_target_pairs={{0,32},{16,48},{32,0},{48,16},{64,96},{80,112},{96,64},{112,80},{1... | collective-permute-start | bytes 98312 | tf_op jit(solution)/shard_map/ppermute | solution.py:263
  59.9 8.2 %collective-permute-start.9 = (bf16[64,256]{1,0:T(8,128)(2,1)S(1)}, bf16[64,256]{1,0:T(8,128)(2,1)S(1)}, u32[]{:S(2)}, u32[]{:S(2)}) collective-permute-start(bf16[64,256]{1,0:T(8,128)(2,1)S(1)} %get-tuple-element.34), channel_id=1, source_target_pairs={{0,64},{16,80},{32,96},{48,112},{64,0},{80,16},{96,32},{112,48},{1... | collective-permute-start | bytes 98312 | tf_op jit(solution)/shard_map/ppermute | solution.py:263
  61.0 11.0 %collective-permute-start.10 = (bf16[64,256]{1,0:T(8,128)(2,1)S(1)}, bf16[64,256]{1,0:T(8,128)(2,1)S(1)}, u32[]{:S(2)}, u32[]{:S(2)}) collective-permute-start(bf16[64,256]{1,0:T(8,128)(2,1)S(1)} %get-tuple-element.35), channel_id=1, source_target_pairs={{0,96},{16,112},{32,64},{48,80},{64,32},{80,48},{96,0},{112,16},{1... | collective-permute-start | bytes 98312 | tf_op jit(solution)/shard_map/ppermute | solution.py:263
  62.7 9.3 %collective-permute-start.11 = (bf16[64,256]{1,0:T(8,128)(2,1)S(1)}, bf16[64,256]{1,0:T(8,128)(2,1)S(1)}, u32[]{:S(2)}, u32[]{:S(2)}) collective-permute-start(bf16[64,256]{1,0:T(8,128)(2,1)S(1)} %get-tuple-element.36), channel_id=1, source_target_pairs={{0,128},{16,144},{32,160},{48,176},{64,192},{80,208},{96,224},{112... | collective-permute-start | bytes 98312 | tf_op jit(solution)/shard_map/ppermute | solution.py:263
  64.8 7.8 %collective-permute-start.12 = (bf16[64,256]{1,0:T(8,128)(2,1)S(1)}, bf16[64,256]{1,0:T(8,128)(2,1)S(1)}, u32[]{:S(2)}, u32[]{:S(2)}) collective-permute-start(bf16[64,256]{1,0:T(8,128)(2,1)S(1)} %get-tuple-element.37), channel_id=1, source_target_pairs={{0,160},{16,176},{32,128},{48,144},{64,224},{80,240},{96,192},{112... | collective-permute-start | bytes 98312 | tf_op jit(solution)/shard_map/ppermute | solution.py:263
  67.8 5.1 %collective-permute-start.13 = (bf16[64,256]{1,0:T(8,128)(2,1)S(1)}, bf16[64,256]{1,0:T(8,128)(2,1)S(1)}, u32[]{:S(2)}, u32[]{:S(2)}) collective-permute-start(bf16[64,256]{1,0:T(8,128)(2,1)S(1)} %get-tuple-element.38), channel_id=1, source_target_pairs={{0,192},{16,208},{32,224},{48,240},{64,128},{80,144},{96,160},{112... | collective-permute-start | bytes 98312 | tf_op jit(solution)/shard_map/ppermute | solution.py:263
  68.1 7.5 %collective-permute-start.14 = (bf16[64,256]{1,0:T(8,128)(2,1)S(1)}, bf16[64,256]{1,0:T(8,128)(2,1)S(1)}, u32[]{:S(2)}, u32[]{:S(2)}) collective-permute-start(bf16[64,256]{1,0:T(8,128)(2,1)S(1)} %get-tuple-element.39), channel_id=1, source_target_pairs={{0,224},{16,240},{32,192},{48,208},{64,160},{80,176},{96,128},{112... | collective-permute-start | bytes 98312 | tf_op jit(solution)/shard_map/ppermute | solution.py:263
  75.6 1.6 %copy-start = (f32[512,1024]{1,0:T(8,128)S(1)}, f32[512,1024]{1,0:T(8,128)}, u32[]{:S(2)}) copy-start(f32[512,1024]{1,0:T(8,128)} %get-tuple-element.23.resid_hbm) | copy-start | bytes 6291460

commit v3 on v2

--- a/solution.py
+++ b/solution.py
@@ -67,18 +67,19 @@
     counts_hbm, x_hbm, g1_hbm, g2_hbm, w1_hbm, w2_hbm, w3_hbm, me_ref,
     resid_hbm, row_hbm, *refs,
 ):
-    chips = 8
-    cols_hbm = refs[:chips]
+    chips = 4
+    cols_hbm, kv_hbm = refs[:chips], refs[chips]
     (
         counts, x_ref, g1_ref, g2_ref, w1, w2, w3, normed, qkv, heads,
         resid_ref, row_ref, col_ref, wide, sems, wsems, osems,
-    ) = refs[chips:]
+    ) = refs[chips + 1 :]
     prows, row_flat, _ = row_ref.shape
     tokens, width = resid_ref.shape
     slots = x_hbm.shape[2]
     pcols = x_hbm.shape[1]
     inner = HB * HD
-    chip = me_ref[0] // 2
+    each_slots = slots // chips
+    chip = me_ref[0] // 4
     small = [
         pltpu.make_async_copy(g1_hbm, g1_ref, sems.at[1]),
         pltpu.make_async_copy(g2_hbm, g2_ref, sems.at[2]),
@@ -156,8 +157,8 @@
         wide[i % 2, 0] = w[:, :128]
         wide[i % 2, 1] = w[:, 128:]
         for d in range(chips):
-            for low in range(2):
-                s = 2 * (chip ^ d) + low
+            for low in range(each_slots):
+                s = each_slots * (chip ^ d) + low
                 for c in range(pcols):
                     part = [
                         wide[i % 2, j, pl.ds(c * slots + s, prows, stride=pcols * slots), :]
@@ -168,12 +169,15 @@
     for d in range(chips):
         stores.append(pltpu.make_async_copy(col_ref.at[d], cols_hbm[d], osems.at[1 + d]))
         stores[-1].start()
+    kv = pl.ds(HC * HD, 2 * HC * HD)
+    stores.append(pltpu.make_async_copy(col_ref.at[0, :, kv], kv_hbm, osems.at[1 + chips]))
+    stores[-1].start()
     for i in range(3):
         to = pl.ds(i * 256, 256)
         r = dot(normed[...], w3[:, pl.ds(i * inner, 256)]).astype(BF16)
         row_ref[:, :, to] = r.reshape(prows, row_flat, 256)
         stores.append(
-            pltpu.make_async_copy(row_ref.at[:, :, to], row_hbm.at[:, :, to], osems.at[1 + chips + i])
+            pltpu.make_async_copy(row_ref.at[:, :, to], row_hbm.at[:, :, to], osems.at[2 + chips + i])
         )
         stores[-1].start()
     for c in stores:
@@ -198,39 +202,38 @@
     o_ref[...] = flat[...].reshape(n, each, HR * HD)
 
 
-def col_kernel(own_ref, cross_ref, *refs):
-    n = len(refs) // 2
-    pieces, outs = (own_ref,) + refs[:n], refs[n:]
+def col_kernel(*refs):
+    n = 4
+    pieces, others, outs = refs[:n], refs[n : 4 * n], refs[4 * n :]
     prows = 16
-    each = cross_ref.shape[1]
-    others = [cross_ref.at[d] for d in range(len(pieces))]
+    each = pieces[0].shape[0]
     for g in range(each // prows):
         part = pl.ds(g * prows, prows)
 
         def take(refs_, at):
-            return jnp.concatenate([r[part, pl.ds(at, 128)] for r in refs_], axis=0)
+            return [r[part, pl.ds(at, 128)] for r in refs_]
 
         for t in range(HC // 2):
             at = t * 128
-            k = halves(jnp.concatenate([take(pieces, 256 + at), take(others, at)], axis=0))
-            v = with_ones(halves(jnp.concatenate([take(pieces, 512 + at), take(others, 256 + at)], axis=0)))
-            o = pair_attention(take(pieces, at), k, v, None)
-            for d in range(len(pieces)):
+            k = jnp.concatenate(take(pieces, 256 + at) + take(others, at), axis=0)
+            v = jnp.concatenate(take(pieces, 512 + at) + take(others, 256 + at), axis=0)
+            q = jnp.concatenate(take(pieces, at), axis=0)
+            o = pair_attention(q, halves(k), with_ones(halves(v)), None)
+            for d in range(n):
                 outs[d][part, pl.ds(at, 128)] = o[d * prows : (d + 1) * prows]
 
 
-def mid_kernel(me_ref, resid_hbm, *refs):
-    pieces, (w_ref, acc_ref, wide, natural, resid_ref, rsems) = refs[:8], refs[8:]
+def mid_kernel(me_ref, resid_hbm, p0, p1, p2, p3, w_ref, acc_ref, wide, natural, resid_ref, rsems):
+    pieces = (p0, p1, p2, p3)
     loads = []
     for t in range(acc_ref.shape[1] // 256):
         cols = pl.ds(t * 256, 256)
         loads.append(pltpu.make_async_copy(resid_hbm.at[:, cols], resid_ref.at[:, cols], rsems.at[t]))
         loads[t].start()
-    slots = 2 * len(pieces)
+    slots = prows = 16
     each = pieces[0].shape[0]
-    prows = 16
-    pcols = each // 2 // prows
-    chip = me_ref[0] // 2
+    pcols = each * len(pieces) // slots // prows
+    chip = me_ref[0] // 4
     for d in range(len(pieces)):
         to = pl.ds(pl.multiple_of((chip ^ d) * each, each), each)
         for j in range(2):
@@ -247,12 +250,19 @@
         acc_ref[:, cols] = resid_ref[:, cols] + dot(natural[...], w_ref[:, cols])
 
 
-def last_kernel(acc_ref, row_ref, w_ref, out_ref):
+def last_kernel(acc_ref, row_ref, w_ref, out_hbm, out_ref, sems):
     m = acc_ref.shape[0]
-    heads = row_ref[...].reshape(m, row_ref.shape[2])
-    for t in range(acc_ref.shape[1] // 256):
-        cols = pl.ds(t * 256, 256)
-        out_ref[:, cols] = (acc_ref[:, cols] + dot(heads, w_ref[:, cols])).astype(BF16)
+    n = sems.shape[0]
+    stores = []
+    for i in range(n):
+        rows = pl.ds(i * (m // n), m // n)
+        heads = row_ref[pl.ds(i * (row_ref.shape[0] // n), row_ref.shape[0] // n)]
+        heads = heads.reshape(m // n, row_ref.shape[2])
+        out_ref[rows, :] = (acc_ref[rows, :] + dot(heads, w_ref[...])).astype(BF16)
+        stores.append(pltpu.make_async_copy(out_ref.at[rows], out_hbm.at[rows], sems.at[i]))
+        stores[i].start()
+    for c in stores:
+        c.wait()
 
 
 def cost(flops, nbytes, trans=0):
@@ -268,21 +278,23 @@
     m = prows * pcols * slots
     inner = HB * HD
     wide = 3 * HR * HD
-    half = slots // 2
-    each = 2 * pcols * prows
+    xn = 4
+    each = slots // xn * pcols * prows
+    kv_wide = 2 * HC * HD
     rows_axes = ("band", "row")
     me = lax.axis_index(rows_axes).astype(jnp.int32).reshape(1)
 
     def params(mib):
         return pltpu.CompilerParams(vmem_limit_bytes=mib << 20)
 
-    resid, row_qkv, *col_qkv = pl.pallas_call(
+    resid, row_qkv, *col_qkv, kv0 = pl.pallas_call(
         local_kernel,
         name="local",
         out_shape=(jax.ShapeDtypeStruct((m, width), F32), jax.ShapeDtypeStruct((prows, pcols * slots, wide), BF16))
-        + (jax.ShapeDtypeStruct((each, wide), BF16),) * half,
+        + (jax.ShapeDtypeStruct((each, wide), BF16),) * xn
+        + (jax.ShapeDtypeStruct((each, kv_wide), BF16),),
         in_specs=[HBM] * 7 + [SMEM],
-        out_specs=(HBM,) * (2 + half),
+        out_specs=(HBM,) * (3 + xn),
         scratch_shapes=[
             pltpu.SMEM(counts.shape, jnp.int32),
             pltpu.VMEM(tokens.shape, BF16),
@@ -296,21 +308,25 @@
             pltpu.VMEM((m, inner), BF16),
             pltpu.VMEM((m, width), F32),
             pltpu.VMEM((prows, pcols * slots, wide), BF16),
-            pltpu.VMEM((half, each, wide), BF16),
+            pltpu.VMEM((xn, each, wide), BF16),
             pltpu.VMEM((2, 2, m, 128), F32),
             pltpu.SemaphoreType.DMA((7,)),
             pltpu.SemaphoreType.DMA((7,)),
-            pltpu.SemaphoreType.DMA((4 + half,)),
+            pltpu.SemaphoreType.DMA((5 + xn,)),
         ],
         compiler_params=params(59),
         cost_estimate=cost(2 * m * width * 4096, 12 << 20),
     )(counts, tokens, norm_band, norm_space, w_band_qkv, w_band_out, w_space_qkv, me)
     row_all = lax.all_to_all(row_qkv, "col", 0, 0, tiled=True)
-    got = []
-    for d in range(1, half):
-        got.append(flip(col_qkv[d], rows_axes, slots, 2 * d))
-    pack = jnp.stack([g[:, HC * HD :] for g in [col_qkv[0]] + got])
-    cross = flip(pack, rows_axes, slots, 1)
+    pieces, kvs = [col_qkv[0]], [kv0]
+    for d in range(1, xn):
+        pieces.append(flip(col_qkv[d], rows_axes, slots, 4 * d))
+        kvs.append(pieces[d][:, HC * HD :])
+    far, core, core_far = [], [], []
+    for d in range(xn):
+        far.append(flip(kvs[d], rows_axes, slots, 2))
+        core.append(flip(kvs[d], rows_axes, slots, 1))
+        core_far.append(flip(far[d], rows_axes, slots, 1))
     row_o = pl.pallas_call(
         row_kernel,
         name="row_attention",
@@ -324,34 +340,35 @@
     col_o = pl.pallas_call(
         col_kernel,
         name="column_attention",
-        out_shape=(jax.ShapeDtypeStruct((each, HC * HD), BF16),) * half,
-        in_specs=[VMEM] * (half + 1),
-        out_specs=(VMEM,) * half,
+        out_shape=(jax.ShapeDtypeStruct((each, HC * HD), BF16),) * xn,
+        in_specs=[VMEM] * (4 * xn),
+        out_specs=(VMEM,) * xn,
         compiler_params=params(16),
         cost_estimate=cost(1 << 28, 1 << 20),
-    )(col_qkv[0], cross, *got)
+    )(*pieces, *far, *core, *core_far)
     back = [col_o[0]]
-    for d in range(1, half):
-        back.append(flip(col_o[d], rows_axes, slots, 2 * d))
+    for d in range(1, xn):
+        back.append(flip(col_o[d], rows_axes, slots, 4 * d))
     acc = pl.pallas_call(
         mid_kernel,
         name="column_projection",
         out_shape=jax.ShapeDtypeStruct((m, width), F32),
-        in_specs=[SMEM, HBM] + [VMEM] * half + [VMEM], out_specs=VMEM,
+        in_specs=[SMEM, HBM] + [VMEM] * (xn + 1), out_specs=VMEM,
         scratch_shapes=[
             pltpu.VMEM((2, m, 128), F32),
             pltpu.VMEM((m, HC * HD), BF16),
             pltpu.VMEM((m, width), F32),
             pltpu.SemaphoreType.DMA((width // 256,)),
         ],
-        compiler_params=params(16),
+        compiler_params=params(50),
         cost_estimate=cost(2 * m * width * 256, 5 << 20),
     )(me, resid, *back, w_space_out[HR * HD :])
     out = pl.pallas_call(
         last_kernel,
         name="row_projection",
         out_shape=jax.ShapeDtypeStruct((m, width), BF16),
-        in_specs=[VMEM, VMEM, VMEM], out_specs=VMEM,
+        in_specs=[VMEM, VMEM, VMEM], out_specs=HBM,
+        scratch_shapes=[pltpu.VMEM((m, width), BF16), pltpu.SemaphoreType.DMA((4,))],
         compiler_params=params(16),
         cost_estimate=cost(2 * m * width * 256, 5 << 20),
     )(acc, row_heads, w_space_out[: HR * HD])

time: 81.4 us -> 68.9 us (0.85)
  starting transfers between devices: 51.9 us -> 40.1 us
  local copies, waits for them, and re-layouts: 7.54 us -> 1.3 us
  waiting for transfers between devices: 5.54 us -> 10.1 us
  Pallas kernels: 15.6 us -> 16.5 us
    ppermute x15 -> x18, starting transfers between devices: 34.6 us -> 21.6 us  [flip(): return lax.ppermute(array, axes, [(i, i ^ by) for i in range(n)])]
    unnamed x13 -> x2, local copies, waits for them, and re-layouts: 6.85 us -> 0.01 us
    ppermute x15 -> x18, waiting for transfers between devices: 5.53 us -> 9.92 us  [flip(): return lax.ppermute(array, axes, [(i, i ^ by) for i in range(n)])]
    all_to_all x1, starting transfers between devices: 7.52 us -> 8.72 us  [local(): row_heads = lax.all_to_all(row_o, 'col', 0, 0, tiled=True)]
    slice x1, local copies, waits for them, and re-layouts: 0.07 us -> 1.27 us  [local(): w_space_out[:HR * HD]]
    pallas_call x1, Pallas kernels: 0.92 us -> 1.74 us  [local(): pl.pallas_call(col_kernel, name='column_attention', out_shape=(jax.ShapeD...]
  transfers between devices with their start and end apart: 17 -> 20, of which waited for: 4 -> 9; matrix products, arithmetic and copies ran while one was open for 7% -> 2% of each run, Pallas kernels for 7% -> 9%
where the time goes in v3:
time: 68.9 us; the launch traced here: 68.2 us
  starting transfers between devices  40.1 us (58%)
  Pallas kernels  16.5 us (24%)
  waiting for transfers between devices  10.1 us (15%)
  local copies, waits for them, and re-layouts  1.3 us (2%)
    ppermute x18, starting transfers between devices, flip(): return lax.ppermute(array, axes, [(i, i ^ by) for i in range(n)])  21.6 us
    ppermute x18, waiting for transfers between devices, flip(): return lax.ppermute(array, axes, [(i, i ^ by) for i in range(n)])  9.92 us
    all_to_all x1, starting transfers between devices, local(): row_all = lax.all_to_all(row_qkv, 'col', 0, 0, tiled=True)  9.74 us
    pallas_call x1, Pallas kernels, local(): pl.pallas_call(local_kernel, name='local', out_shape=(jax.ShapeDtypeStruc...  8.93 us
    all_to_all x1, starting transfers between devices, local(): row_heads = lax.all_to_all(row_o, 'col', 0, 0, tiled=True)  8.72 us
    pallas_call x1, Pallas kernels, local(): pl.pallas_call(row_kernel, name='row_attention', out_shape=jax.ShapeDtype...  2.32 us
    pallas_call x1, Pallas kernels, local(): pl.pallas_call(mid_kernel, name='column_projection', out_shape=jax.ShapeD...  2.22 us
    pallas_call x1, Pallas kernels, local(): pl.pallas_call(col_kernel, name='column_attention', out_shape=(jax.ShapeD...  1.74 us
  transfers between devices with their start and end apart: 20, of which 9 were waited for; matrix products, arithmetic and copies ran while one was open for 2% of the time, Pallas kernels for 9%

profile of v3, /device:TPU:32, one launch (start us, length us, event | category | flops | bytes accessed | tf_op | source)
XLA Modules:
  0.0 68.2 jit_solution(8911192320192756365)
XLA Ops:
  0.0 8.9 %local.1 = (f32[512,1024]{1,0:T(8,128)}, bf16[16,32,768]{2,1,0:T(8,128)(2,1)}, bf16[128,768]{1,0:T(8,128)(2,1)}, bf16[128,768]{1,0:T(8,128)(2,1)}, bf16[128,768]...) custom-call(s32[4]{0:T(128)} %counts_hbm.1, bf16[16,2,16,1024]{3,2,1,0:T(8,128)(2,1)} %x_hbm.1, ...), custom_call_target="tpu_custom_call" | custom-call | flops 4294967296 | bytes 12582912 | tf_op jit(solution)/shard_map/local/pallas_call | solution.py:290
  8.9 0.0 copy-start
  9.0 9.7 %all-to-all-start = ((bf16[16,32,768]{2,1,0:T(8,128)(2,1)}), bf16[16,32,768]{2,1,0:T(8,128)(2,1)S(1)}, u32[]{:S(2)}, u32[]{:S(2)}) async-start(bf16[16,32,768]{2,1,0:T(8,128)(2,1)} %get-tuple-element.26), calls=%async_computation | async-start | bytes 1572864 | tf_op jit(solution)/shard_map/all_to_all | solution.py:320
  18.7 1.5 %collective-permute-start = (bf16[128,768]{1,0:T(8,128)(2,1)}, bf16[128,768]{1,0:T(8,128)(2,1)S(1)}, u32[]{:S(2)}, u32[]{:S(2)}) collective-permute-start(bf16[128,768]{1,0:T(8,128)(2,1)} %get-tuple-element.18), channel_id=1, source_target_pairs={{0,64},{16,80},{32,96},{48,112},{64,0},{80,16},{96,32},{112,48},{1... | collective-permute-start | bytes 589832 | tf_op jit(solution)/shard_map/ppermute | solution.py:273
  20.2 2.8 %collective-permute-start.1 = (bf16[128,768]{1,0:T(8,128)(2,1)}, bf16[128,768]{1,0:T(8,128)(2,1)S(1)}, u32[]{:S(2)}, u32[]{:S(2)}) collective-permute-start(bf16[128,768]{1,0:T(8,128)(2,1)} %get-tuple-element.19), channel_id=1, source_target_pairs={{0,128},{16,144},{32,160},{48,176},{64,192},{80,208},{96,224},{112... | collective-permute-start | bytes 589832 | tf_op jit(solution)/shard_map/ppermute | solution.py:273
  23.0 0.4 collective-permute-start.2
  23.4 2.9 %collective-permute-start.3 = (bf16[128,512]{1,0:T(8,128)(2,1)}, bf16[128,512]{1,0:T(8,128)(2,1)S(1)}, u32[]{:S(2)}, u32[]{:S(2)}) collective-permute-start(bf16[128,512]{1,0:T(8,128)(2,1)} %get-tuple-element.21), channel_id=1, source_target_pairs={{0,32},{16,48},{32,0},{48,16},{64,96},{80,112},{96,64},{112,80},{1... | collective-permute-start | bytes 393224 | tf_op jit(solution)/shard_map/ppermute | solution.py:273
  26.3 0.0 collective-permute-start.7
  26.3 4.9 %collective-permute-done.3.refs_4_ = bf16[128,512]{1,0:T(8,128)(2,1)S(1)} collective-permute-done((bf16[128,512]{1,0:T(8,128)(2,1)}, bf16[128,512]{1,0:T(8,128)(2,1)S(1)}, u32[]{:S(2)}, u32[]{:S(2)}) %collective-permute-start.3) | collective-permute-done | bytes 131104 | tf_op jit(solution)/shard_map/ppermute | solution.py:273
  31.2 0.0 collective-permute-start.11
  31.2 0.0 collective-permute-done.refs_1_
  31.2 0.6 collective-permute-start.8
  31.8 0.0 collective-permute-done.1.refs_2_
  31.8 3.5 %collective-permute-start.4 = (bf16[128,512]{1,0:T(8,128)(2,1)S(1)}, bf16[128,512]{1,0:T(8,128)(2,1)S(1)}, u32[]{:S(2)}, u32[]{:S(2)}) collective-permute-start(bf16[128,512]{1,0:T(8,128)(2,1)S(1)} %slice.20), channel_id=1, source_target_pairs={{0,32},{16,48},{32,0},{48,16},{64,96},{80,112},{96,64},{112,80},{1... | collective-permute-start | bytes 393224 | tf_op jit(solution)/shard_map/ppermute | solution.py:273
  35.4 0.0 collective-permute-done.2.refs_3_
  35.4 1.6 %collective-permute-start.5 = (bf16[128,512]{1,0:T(8,128)(2,1)S(1)}, bf16[128,512]{1,0:T(8,128)(2,1)S(1)}, u32[]{:S(2)}, u32[]{:S(2)}) collective-permute-start(bf16[128,512]{1,0:T(8,128)(2,1)S(1)} %slice.21), channel_id=1, source_target_pairs={{0,32},{16,48},{32,0},{48,16},{64,96},{80,112},{96,64},{112,80},{1... | collective-permute-start | bytes 393224 | tf_op jit(solution)/shard_map/ppermute | solution.py:273
  37.0 0.0 collective-permute-done.7.refs_8_
  37.0 2.3 %collective-permute-start.6 = (bf16[128,512]{1,0:T(8,128)(2,1)S(1)}, bf16[128,512]{1,0:T(8,128)(2,1)S(1)}, u32[]{:S(2)}, u32[]{:S(2)}) collective-permute-start(bf16[128,512]{1,0:T(8,128)(2,1)S(1)} %slice.22), channel_id=1, source_target_pairs={{0,32},{16,48},{32,0},{48,16},{64,96},{80,112},{96,64},{112,80},{1... | collective-permute-start | bytes 393224 | tf_op jit(solution)/shard_map/ppermute | solution.py:273
  39.3 0.2 all-to-all-done.x_ref
  39.5 2.3 %row_attention.1 = bf16[16,32,256]{2,1,0:T(8,128)(2,1)} custom-call(bf16[16,32,768]{2,1,0:T(8,128)(2,1)S(1)} %all-to-all-done.x_ref), custom_call_target="tpu_custom_call" | custom-call | flops 536870912 | bytes 1048576 | tf_op jit(solution)/shard_map/row_attention/pallas_call | solution.py:330
  41.8 8.7 %all-to-all-start.1 = ((bf16[16,32,256]{2,1,0:T(8,128)(2,1)}), bf16[16,32,256]{2,1,0:T(8,128)(2,1)S(1)}, u32[]{:S(2)}, u32[]{:S(2)}) async-start(bf16[16,32,256]{2,1,0:T(8,128)(2,1)} %row_attention.1), calls=%async_computation.1 | async-start | bytes 524288 | tf_op jit(solution)/shard_map/all_to_all | solution.py:339
  50.5 0.0 collective-permute-done.11.refs_12_
  50.5 0.1 collective-permute-start.9
  50.6 0.0 collective-permute-done.8.refs_9_
  50.6 0.5 collective-permute-start.10
  51.1 0.0 collective-permute-done.4.refs_5_
  51.1 0.1 collective-permute-start.12
  51.2 0.0 collective-permute-done.5.refs_6_
  51.2 0.4 collective-permute-start.13
  51.6 0.0 collective-permute-done.6.refs_7_
  51.6 0.1 collective-permute-start.14
  51.7 0.2 collective-permute-done.9.refs_10_
  52.0 0.2 collective-permute-done.10.refs_11_
  52.1 0.3 collective-permute-done.12.refs_13_
  52.5 0.2 collective-permute-done.13.refs_14_
  52.7 0.3 collective-permute-done.14.refs_15_
  53.0 0.0 copy-done
  53.0 1.7 %column_attention.1 = (bf16[128,256]{1,0:T(8,128)(2,1)S(1)}, bf16[128,256]{1,0:T(8,128)(2,1)S(1)}, bf16[128,256]{1,0:T(8,128)(2,1)S(1)}, bf16[128,256]{1,0:T(8,128)(2,1)S(1)}) custom-call(bf16[128,768]{1,0:T(8,128)(2,1)S(1)} %copy-done, bf16[128,768]{1,0:T(8,128)(2,1)S(1)} %collective-permute-done.refs_1_, ...), custom_call_target="tpu_custom_call" | custom-call | flops 268435456 | bytes 1048576 | tf_op jit(solution)/shard_map/column_attention/pallas_call | solution.py:340
  54.7 0.1 collective-permute-start.15
  54.8 4.2 %collective-permute-start.16 = (bf16[128,256]{1,0:T(8,128)(2,1)S(1)}, bf16[128,256]{1,0:T(8,128)(2,1)S(1)}, u32[]{:S(2)}, u32[]{:S(2)}) collective-permute-start(bf16[128,256]{1,0:T(8,128)(2,1)S(1)} %get-tuple-element.24), channel_id=1, source_target_pairs={{0,128},{16,144},{32,160},{48,176},{64,192},{80,208},{96,224},{112... | collective-permute-start | bytes 196616 | tf_op jit(solution)/shard_map/ppermute | solution.py:273
  59.1 0.4 collective-permute-start.17
  59.5 1.3 %fusion = (bf16[256,1024]{1,0:T(8,128)(2,1)S(1)}, bf16[256,1024]{1,0:T(8,128)(2,1)S(1)}) fusion(bf16[512,1024]{1,0:T(8,128)(2,1)} %param.15), kind=kLoop, calls=%fused_computation | loop fusion | bytes 2097152 | tf_op jit(solution)/shard_map/slice | solution.py:374
  60.8 0.0 collective-permute-done.15.p1
  60.8 1.8 %collective-permute-done.16.p2 = bf16[128,256]{1,0:T(8,128)(2,1)S(1)} collective-permute-done((bf16[128,256]{1,0:T(8,128)(2,1)S(1)}, bf16[128,256]{1,0:T(8,128)(2,1)S(1)}, u32[]{:S(2)}, u32[]{:S(2)}) %collective-permute-start.16) | collective-permute-done | bytes 65568 | tf_op jit(solution)/shard_map/ppermute | solution.py:273
  62.7 1.9 %collective-permute-done.17.p3 = bf16[128,256]{1,0:T(8,128)(2,1)S(1)} collective-permute-done((bf16[128,256]{1,0:T(8,128)(2,1)S(1)}, bf16[128,256]{1,0:T(8,128)(2,1)S(1)}, u32[]{:S(2)}, u32[]{:S(2)}) %collective-permute-start.17) | collective-permute-done | bytes 65568 | tf_op jit(solution)/shard_map/ppermute | solution.py:273
  64.6 2.2 %column_projection.1.acc_ref = f32[512,1024]{1,0:T(8,128)S(1)} custom-call(s32[1]{0:T(128)} %bitcast.me_ref, f32[512,1024]{1,0:T(8,128)} %get-tuple-element.16.resid_hbm, bf16[128,256]{1,0:T(8,128)(2,1)S(1)} %get-tuple-element.22.p0, bf16[128,256]{1,0:T(8,128)(2,1)S(1)} %collective-permute-done.15.p1, bf16[128,256]{1,0:T(8,128)(2,1)S(1)} %collective-permute-done.16.p2, ...), custom_call_target="tpu_custom_call" | custom-call | flops 268435456 | bytes 5242880 | tf_op jit(solution)/shard_map/column_projection/pallas_call | solution.py:352
  66.8 0.0 all-to-all-done.1.row_ref
  66.8 1.2 %row_projection.1 = bf16[512,1024]{1,0:T(8,128)(2,1)} custom-call(f32[512,1024]{1,0:T(8,128)S(1)} %column_projection.1.acc_ref, bf16[16,32,256]{2,1,0:T(8,128)(2,1)S(1)} %all-to-all-done.1.row_ref, bf16[256,1024]{1,0:T(8,128)(2,1)S(1)} %get-tuple-element.27.w_ref), custom_call_target="tpu_custom_call" | custom-call | flops 268435456 | bytes 5242880 | tf_op jit(solution)/shard_map/row_projection/pallas_call | solution.py:366
  (3 shorter events, 0.0 us)
Async XLA Ops:
  8.9 44.0 %copy-start = (bf16[128,768]{1,0:T(8,128)(2,1)S(1)}, bf16[128,768]{1,0:T(8,128)(2,1)}, u32[]{:S(2)}) copy-start(bf16[128,768]{1,0:T(8,128)(2,1)} %get-tuple-element.17.refs_0_) | copy-start | bytes 589828
  9.0 30.5 %all-to-all-start = ((bf16[16,32,768]{2,1,0:T(8,128)(2,1)}), bf16[16,32,768]{2,1,0:T(8,128)(2,1)S(1)}, u32[]{:S(2)}, u32[]{:S(2)}) async-start(bf16[16,32,768]{2,1,0:T(8,128)(2,1)} %get-tuple-element.26), calls=%async_computation | async-start | bytes 1572864 | tf_op jit(solution)/shard_map/all_to_all | solution.py:320
  18.7 12.5 %collective-permute-start = (bf16[128,768]{1,0:T(8,128)(2,1)}, bf16[128,768]{1,0:T(8,128)(2,1)S(1)}, u32[]{:S(2)}, u32[]{:S(2)}) collective-permute-start(bf16[128,768]{1,0:T(8,128)(2,1)} %get-tuple-element.18), channel_id=1, source_target_pairs={{0,64},{16,80},{32,96},{48,112},{64,0},{80,16},{96,32},{112,48},{1... | collective-permute-start | bytes 589832 | tf_op jit(solution)/shard_map/ppermute | solution.py:273
  20.2 11.6 %collective-permute-start.1 = (bf16[128,768]{1,0:T(8,128)(2,1)}, bf16[128,768]{1,0:T(8,128)(2,1)S(1)}, u32[]{:S(2)}, u32[]{:S(2)}) collective-permute-start(bf16[128,768]{1,0:T(8,128)(2,1)} %get-tuple-element.19), channel_id=1, source_target_pairs={{0,128},{16,144},{32,160},{48,176},{64,192},{80,208},{96,224},{112... | collective-permute-start | bytes 589832 | tf_op jit(solution)/shard_map/ppermute | solution.py:273
  23.0 12.4 %collective-permute-start.2 = (bf16[128,768]{1,0:T(8,128)(2,1)}, bf16[128,768]{1,0:T(8,128)(2,1)S(1)}, u32[]{:S(2)}, u32[]{:S(2)}) collective-permute-start(bf16[128,768]{1,0:T(8,128)(2,1)} %get-tuple-element.20), channel_id=1, source_target_pairs={{0,192},{16,208},{32,224},{48,240},{64,128},{80,144},{96,160},{112... | collective-permute-start | bytes 589832 | tf_op jit(solution)/shard_map/ppermute | solution.py:273
  23.4 7.8 %collective-permute-start.3 = (bf16[128,512]{1,0:T(8,128)(2,1)}, bf16[128,512]{1,0:T(8,128)(2,1)S(1)}, u32[]{:S(2)}, u32[]{:S(2)}) collective-permute-start(bf16[128,512]{1,0:T(8,128)(2,1)} %get-tuple-element.21), channel_id=1, source_target_pairs={{0,32},{16,48},{32,0},{48,16},{64,96},{80,112},{96,64},{112,80},{1... | collective-permute-start | bytes 393224 | tf_op jit(solution)/shard_map/ppermute | solution.py:273
  26.3 10.7 %collective-permute-start.7 = (bf16[128,512]{1,0:T(8,128)(2,1)}, bf16[128,512]{1,0:T(8,128)(2,1)S(1)}, u32[]{:S(2)}, u32[]{:S(2)}) collective-permute-start(bf16[128,512]{1,0:T(8,128)(2,1)} %get-tuple-element.21), channel_id=1, source_target_pairs={{0,16},{16,0},{32,48},{48,32},{64,80},{80,64},{96,112},{112,96},{1... | collective-permute-start | bytes 393224 | tf_op jit(solution)/shard_map/ppermute | solution.py:273
  31.2 19.3 %collective-permute-start.11 = (bf16[128,512]{1,0:T(8,128)(2,1)S(1)}, bf16[128,512]{1,0:T(8,128)(2,1)S(1)}, u32[]{:S(2)}, u32[]{:S(2)}) collective-permute-start(bf16[128,512]{1,0:T(8,128)(2,1)S(1)} %collective-permute-done.3.refs_4_), channel_id=1, source_target_pairs={{0,16},{16,0},{32,48},{48,32},{64,80},{80,64},{96,112},{112,96},{1... | collective-permute-start | bytes 393224 | tf_op jit(solution)/shard_map/ppermute | solution.py:273
  31.2 19.4 %collective-permute-start.8 = (bf16[128,512]{1,0:T(8,128)(2,1)S(1)}, bf16[128,512]{1,0:T(8,128)(2,1)S(1)}, u32[]{:S(2)}, u32[]{:S(2)}) collective-permute-start(bf16[128,512]{1,0:T(8,128)(2,1)S(1)} %slice.20), channel_id=1, source_target_pairs={{0,16},{16,0},{32,48},{48,32},{64,80},{80,64},{96,112},{112,96},{1... | collective-permute-start | bytes 393224 | tf_op jit(solution)/shard_map/ppermute | solution.py:273
  31.8 19.3 %collective-permute-start.4 = (bf16[128,512]{1,0:T(8,128)(2,1)S(1)}, bf16[128,512]{1,0:T(8,128)(2,1)S(1)}, u32[]{:S(2)}, u32[]{:S(2)}) collective-permute-start(bf16[128,512]{1,0:T(8,128)(2,1)S(1)} %slice.20), channel_id=1, source_target_pairs={{0,32},{16,48},{32,0},{48,16},{64,96},{80,112},{96,64},{112,80},{1... | collective-permute-start | bytes 393224 | tf_op jit(solution)/shard_map/ppermute | solution.py:273
  35.4 15.9 %collective-permute-start.5 = (bf16[128,512]{1,0:T(8,128)(2,1)S(1)}, bf16[128,512]{1,0:T(8,128)(2,1)S(1)}, u32[]{:S(2)}, u32[]{:S(2)}) collective-permute-start(bf16[128,512]{1,0:T(8,128)(2,1)S(1)} %slice.21), channel_id=1, source_target_pairs={{0,32},{16,48},{32,0},{48,16},{64,96},{80,112},{96,64},{112,80},{1... | collective-permute-start | bytes 393224 | tf_op jit(solution)/shard_map/ppermute | solution.py:273
  37.0 14.7 %collective-permute-start.6 = (bf16[128,512]{1,0:T(8,128)(2,1)S(1)}, bf16[128,512]{1,0:T(8,128)(2,1)S(1)}, u32[]{:S(2)}, u32[]{:S(2)}) collective-permute-start(bf16[128,512]{1,0:T(8,128)(2,1)S(1)} %slice.22), channel_id=1, source_target_pairs={{0,32},{16,48},{32,0},{48,16},{64,96},{80,112},{96,64},{112,80},{1... | collective-permute-start | bytes 393224 | tf_op jit(solution)/shard_map/ppermute | solution.py:273
  41.8 25.0 %all-to-all-start.1 = ((bf16[16,32,256]{2,1,0:T(8,128)(2,1)}), bf16[16,32,256]{2,1,0:T(8,128)(2,1)S(1)}, u32[]{:S(2)}, u32[]{:S(2)}) async-start(bf16[16,32,256]{2,1,0:T(8,128)(2,1)} %row_attention.1), calls=%async_computation.1 | async-start | bytes 524288 | tf_op jit(solution)/shard_map/all_to_all | solution.py:339
  50.5 1.4 %collective-permute-start.9 = (bf16[128,512]{1,0:T(8,128)(2,1)S(1)}, bf16[128,512]{1,0:T(8,128)(2,1)S(1)}, u32[]{:S(2)}, u32[]{:S(2)}) collective-permute-start(bf16[128,512]{1,0:T(8,128)(2,1)S(1)} %slice.21), channel_id=1, source_target_pairs={{0,16},{16,0},{32,48},{48,32},{64,80},{80,64},{96,112},{112,96},{1... | collective-permute-start | bytes 393224 | tf_op jit(solution)/shard_map/ppermute | solution.py:273
  50.6 1.5 %collective-permute-start.10 = (bf16[128,512]{1,0:T(8,128)(2,1)S(1)}, bf16[128,512]{1,0:T(8,128)(2,1)S(1)}, u32[]{:S(2)}, u32[]{:S(2)}) collective-permute-start(bf16[128,512]{1,0:T(8,128)(2,1)S(1)} %slice.22), channel_id=1, source_target_pairs={{0,16},{16,0},{32,48},{48,32},{64,80},{80,64},{96,112},{112,96},{1... | collective-permute-start | bytes 393224 | tf_op jit(solution)/shard_map/ppermute | solution.py:273
  51.1 1.3 %collective-permute-start.12 = (bf16[128,512]{1,0:T(8,128)(2,1)S(1)}, bf16[128,512]{1,0:T(8,128)(2,1)S(1)}, u32[]{:S(2)}, u32[]{:S(2)}) collective-permute-start(bf16[128,512]{1,0:T(8,128)(2,1)S(1)} %collective-permute-done.4.refs_5_), channel_id=1, source_target_pairs={{0,16},{16,0},{32,48},{48,32},{64,80},{80,64},{96,112},{112,96},{1... | collective-permute-start | bytes 393224 | tf_op jit(solution)/shard_map/ppermute | solution.py:273
  51.2 1.4 %collective-permute-start.13 = (bf16[128,512]{1,0:T(8,128)(2,1)S(1)}, bf16[128,512]{1,0:T(8,128)(2,1)S(1)}, u32[]{:S(2)}, u32[]{:S(2)}) collective-permute-start(bf16[128,512]{1,0:T(8,128)(2,1)S(1)} %collective-permute-done.5.refs_6_), channel_id=1, source_target_pairs={{0,16},{16,0},{32,48},{48,32},{64,80},{80,64},{96,112},{112,96},{1... | collective-permute-start | bytes 393224 | tf_op jit(solution)/shard_map/ppermute | solution.py:273
  51.6 1.3 %collective-permute-start.14 = (bf16[128,512]{1,0:T(8,128)(2,1)S(1)}, bf16[128,512]{1,0:T(8,128)(2,1)S(1)}, u32[]{:S(2)}, u32[]{:S(2)}) collective-permute-start(bf16[128,512]{1,0:T(8,128)(2,1)S(1)} %collective-permute-done.6.refs_7_), channel_id=1, source_target_pairs={{0,16},{16,0},{32,48},{48,32},{64,80},{80,64},{96,112},{112,96},{1... | collective-permute-start | bytes 393224 | tf_op jit(solution)/shard_map/ppermute | solution.py:273
  54.7 6.1 %collective-permute-start.15 = (bf16[128,256]{1,0:T(8,128)(2,1)S(1)}, bf16[128,256]{1,0:T(8,128)(2,1)S(1)}, u32[]{:S(2)}, u32[]{:S(2)}) collective-permute-start(bf16[128,256]{1,0:T(8,128)(2,1)S(1)} %get-tuple-element.23), channel_id=1, source_target_pairs={{0,64},{16,80},{32,96},{48,112},{64,0},{80,16},{96,32},{112,48},{1... | collective-permute-start | bytes 196616 | tf_op jit(solution)/shard_map/ppermute | solution.py:273
  54.8 7.8 %collective-permute-start.16 = (bf16[128,256]{1,0:T(8,128)(2,1)S(1)}, bf16[128,256]{1,0:T(8,128)(2,1)S(1)}, u32[]{:S(2)}, u32[]{:S(2)}) collective-permute-start(bf16[128,256]{1,0:T(8,128)(2,1)S(1)} %get-tuple-element.24), channel_id=1, source_target_pairs={{0,128},{16,144},{32,160},{48,176},{64,192},{80,208},{96,224},{112... | collective-permute-start | bytes 196616 | tf_op jit(solution)/shard_map/ppermute | solution.py:273
  59.1 5.5 %collective-permute-start.17 = (bf16[128,256]{1,0:T(8,128)(2,1)S(1)}, bf16[128,256]{1,0:T(8,128)(2,1)S(1)}, u32[]{:S(2)}, u32[]{:S(2)}) collective-permute-start(bf16[128,256]{1,0:T(8,128)(2,1)S(1)} %get-tuple-element.25), channel_id=1, source_target_pairs={{0,192},{16,208},{32,224},{48,240},{64,128},{80,144},{96,160},{112... | collective-permute-start | bytes 196616 | tf_op jit(solution)/shard_map/ppermute | solution.py:273

commit v4 on v3

--- a/solution.py
+++ b/solution.py
@@ -56,6 +56,23 @@
         probs.append(p.astype(BF16))
     mixed = dot(jnp.concatenate(probs, axis=1), vals2)
     return (mixed[:, : 2 * HD] / mixed[:, 2 * HD :]).astype(BF16)
+
+
+def stacked_attention(query, keys, vals, mask):
+    m = query.shape[0]
+    scores = dot_t(halves(query), keys)
+    probs = []
+    for h in range(2):
+        s = scores[h * m : (h + 1) * m]
+        if mask is not None:
+            s = jnp.where(mask, s, NEG)
+        p = jnp.exp2((s - jnp.max(s, axis=-1, keepdims=True)) * SCALE2)
+        probs.append(p.astype(BF16))
+    both = jnp.concatenate([vals, jnp.ones_like(vals)], axis=1)
+    mixed = dot(jnp.concatenate(probs, axis=0), both)
+    low = lax.broadcasted_iota(jnp.int32, (m, 2 * HD), 1) < HD
+    heads = jnp.where(low, mixed[:m, : 2 * HD], mixed[m:, : 2 * HD])
+    return (heads / jnp.where(low, mixed[:m, 2 * HD :], mixed[m:, 2 * HD :])).astype(BF16)
 
 
 def rms(x, gain):
@@ -194,11 +211,11 @@
     mask = rowi % slots == coli % slots
     x = x_ref[...].reshape(m, 3 * HR * HD)
     for t in range(HR // 2):
-        k = halves(x[:, 256 + t * 128 : 384 + t * 128])
-        v = with_ones(halves(x[:, 512 + t * 128 : 640 + t * 128]))
+        k = x[:, 256 + t * 128 : 384 + t * 128]
+        v = x[:, 512 + t * 128 : 640 + t * 128]
         for b in range(m // block):
             q = x[b * block : (b + 1) * block, t * 128 : (t + 1) * 128]
-            flat[pl.ds(b * block, block), pl.ds(t * 128, 128)] = pair_attention(q, k, v, mask)
+            flat[pl.ds(b * block, block), pl.ds(t * 128, 128)] = stacked_attention(q, k, v, mask)
     o_ref[...] = flat[...].reshape(n, each, HR * HD)
 
 
@@ -218,20 +235,33 @@
             k = jnp.concatenate(take(pieces, 256 + at) + take(others, at), axis=0)
             v = jnp.concatenate(take(pieces, 512 + at) + take(others, 256 + at), axis=0)
             q = jnp.concatenate(take(pieces, at), axis=0)
-            o = pair_attention(q, halves(k), with_ones(halves(v)), None)
+            o = stacked_attention(q, k, v, None)
             for d in range(n):
                 outs[d][part, pl.ds(at, 128)] = o[d * prows : (d + 1) * prows]
 
 
-def mid_kernel(me_ref, resid_hbm, p0, p1, p2, p3, w_ref, acc_ref, wide, natural, resid_ref, rsems):
+def row_projection_kernel(resid_hbm, row_ref, w_ref, acc_ref, resid_ref, sems):
+    m = acc_ref.shape[0]
+    n = sems.shape[0]
+    loads = []
+    for i in range(n):
+        rows = pl.ds(i * (m // n), m // n)
+        loads.append(pltpu.make_async_copy(resid_hbm.at[rows], resid_ref.at[rows], sems.at[i]))
+        loads[i].start()
+    each = row_ref.shape[0] // n
+    for i in range(n):
+        rows = pl.ds(i * (m // n), m // n)
+        x = row_ref[pl.ds(i * each, each)].reshape(m // n, row_ref.shape[2])
+        loads[i].wait()
+        acc_ref[rows, :] = resid_ref[rows, :] + dot(x, w_ref[...])
+
+
+def column_projection_kernel(me_ref, acc_ref, p0, p1, p2, p3, w_ref, out_hbm, wide, natural, out_ref, sems):
     pieces = (p0, p1, p2, p3)
-    loads = []
-    for t in range(acc_ref.shape[1] // 256):
-        cols = pl.ds(t * 256, 256)
-        loads.append(pltpu.make_async_copy(resid_hbm.at[:, cols], resid_ref.at[:, cols], rsems.at[t]))
-        loads[t].start()
+    m = acc_ref.shape[0]
+    n = sems.shape[0]
+    each = pieces[0].shape[0]
     slots = prows = 16
-    each = pieces[0].shape[0]
     pcols = each * len(pieces) // slots // prows
     chip = me_ref[0] // 4
     for d in range(len(pieces)):
@@ -244,21 +274,10 @@
                 wide[j, pl.ds(c * prows + r, slots, stride=pcols * prows), :] for j in range(2)
             ]
             natural[pl.ds((r * pcols + c) * slots, slots), :] = jnp.concatenate(part, axis=1).astype(BF16)
-    for t in range(acc_ref.shape[1] // 256):
-        cols = pl.ds(t * 256, 256)
-        loads[t].wait()
-        acc_ref[:, cols] = resid_ref[:, cols] + dot(natural[...], w_ref[:, cols])
-
-
-def last_kernel(acc_ref, row_ref, w_ref, out_hbm, out_ref, sems):
-    m = acc_ref.shape[0]
-    n = sems.shape[0]
     stores = []
     for i in range(n):
         rows = pl.ds(i * (m // n), m // n)
-        heads = row_ref[pl.ds(i * (row_ref.shape[0] // n), row_ref.shape[0] // n)]
-        heads = heads.reshape(m // n, row_ref.shape[2])
-        out_ref[rows, :] = (acc_ref[rows, :] + dot(heads, w_ref[...])).astype(BF16)
+        out_ref[rows, :] = (acc_ref[rows, :] + dot(natural[rows, :], w_ref[...])).astype(BF16)
         stores.append(pltpu.make_async_copy(out_ref.at[rows], out_hbm.at[rows], sems.at[i]))
         stores[i].start()
     for c in stores:
@@ -350,28 +369,28 @@
     for d in range(1, xn):
         back.append(flip(col_o[d], rows_axes, slots, 4 * d))
     acc = pl.pallas_call(
-        mid_kernel,
+        row_projection_kernel,
+        name="row_projection",
+        out_shape=jax.ShapeDtypeStruct((m, width), F32),
+        in_specs=[HBM, VMEM, VMEM], out_specs=VMEM,
+        scratch_shapes=[pltpu.VMEM((m, width), F32), pltpu.SemaphoreType.DMA((4,))],
+        compiler_params=params(50),
+        cost_estimate=cost(2 * m * width * 256, 5 << 20),
+    )(resid, row_heads, w_space_out[: HR * HD])
+    out = pl.pallas_call(
+        column_projection_kernel,
         name="column_projection",
-        out_shape=jax.ShapeDtypeStruct((m, width), F32),
-        in_specs=[SMEM, HBM] + [VMEM] * (xn + 1), out_specs=VMEM,
+        out_shape=jax.ShapeDtypeStruct((m, width), BF16),
+        in_specs=[SMEM] + [VMEM] * (xn + 2), out_specs=HBM,
         scratch_shapes=[
             pltpu.VMEM((2, m, 128), F32),
             pltpu.VMEM((m, HC * HD), BF16),
-            pltpu.VMEM((m, width), F32),
-            pltpu.SemaphoreType.DMA((width // 256,)),
+            pltpu.VMEM((m, width), BF16),
+            pltpu.SemaphoreType.DMA((4,)),
         ],
-        compiler_params=params(50),
-        cost_estimate=cost(2 * m * width * 256, 5 << 20),
-    )(me, resid, *back, w_space_out[HR * HD :])
-    out = pl.pallas_call(
-        last_kernel,
-        name="row_projection",
-        out_shape=jax.ShapeDtypeStruct((m, width), BF16),
-        in_specs=[VMEM, VMEM, VMEM], out_specs=HBM,
-        scratch_shapes=[pltpu.VMEM((m, width), BF16), pltpu.SemaphoreType.DMA((4,))],
         compiler_params=params(16),
         cost_estimate=cost(2 * m * width * 256, 5 << 20),
-    )(acc, row_heads, w_space_out[: HR * HD])
+    )(me, acc, *back, w_space_out[HR * HD :])
     return out.reshape(prows, pcols, slots, width)
 
 

time: 68.9 us -> 65.4 us (0.949)
  starting transfers between devices: 40.1 us -> 38.7 us
  waiting for transfers between devices: 10.1 us -> 8.74 us
  Pallas kernels: 16.5 us -> 15.8 us
    ppermute x18, waiting for transfers between devices: 9.92 us -> 6.6 us  [flip(): return lax.ppermute(array, axes, [(i, i ^ by) for i in range(n)])]
    all_to_all x1, waiting for transfers between devices: 0.01 us -> 1.27 us  [local(): row_heads = lax.all_to_all(row_o, 'col', 0, 0, tiled=True)]
    pallas_call x1, Pallas kernels: 1.74 us -> 0.91 us  [local(): pl.pallas_call(col_kernel, name='column_attention', out_shape=(jax.ShapeD...]
    all_to_all x1, waiting for transfers between devices: 0.18 us -> 0.87 us  [local(): row_all = lax.all_to_all(row_qkv, 'col', 0, 0, tiled=True)]
    all_to_all x1, starting transfers between devices: 8.72 us -> 8.03 us  [local(): row_heads = lax.all_to_all(row_o, 'col', 0, 0, tiled=True)]
  transfers between devices with their start and end apart: 20 -> 20, of which waited for: 9 -> 9; matrix products, arithmetic and copies ran while one was open for 2% -> 2% of each run, Pallas kernels for 9% -> 8%
where the time goes in v4:
time: 65.4 us; the launch traced here: 64.8 us
  starting transfers between devices  38.7 us (59%)
  Pallas kernels  15.8 us (24%)
  waiting for transfers between devices  8.74 us (13%)
  local copies, waits for them, and re-layouts  1.3 us (2%)
    ppermute x18, starting transfers between devices, flip(): return lax.ppermute(array, axes, [(i, i ^ by) for i in range(n)])  20.9 us
    all_to_all x1, starting transfers between devices, local(): row_all = lax.all_to_all(row_qkv, 'col', 0, 0, tiled=True)  9.74 us
    pallas_call x1, Pallas kernels, local(): pl.pallas_call(local_kernel, name='local', out_shape=(jax.ShapeDtypeStruc...  8.93 us
    all_to_all x1, starting transfers between devices, local(): row_heads = lax.all_to_all(row_o, 'col', 0, 0, tiled=True)  8.03 us
    ppermute x18, waiting for transfers between devices, flip(): return lax.ppermute(array, axes, [(i, i ^ by) for i in range(n)])  6.6 us
    pallas_call x1, Pallas kernels, local(): pl.pallas_call(row_kernel, name='row_attention', out_shape=jax.ShapeDtype...  2.39 us
    pallas_call x1, Pallas kernels, local(): pl.pallas_call(row_projection_kernel, name='row_projection', out_shape=ja...  2.04 us
    pallas_call x1, Pallas kernels, local(): pl.pallas_call(column_projection_kernel, name='column_projection', out_sh...  1.52 us
  transfers between devices with their start and end apart: 20, of which 9 were waited for; matrix products, arithmetic and copies ran while one was open for 2% of the time, Pallas kernels for 8%

profile of v4, /device:TPU:32, one launch (start us, length us, event | category | flops | bytes accessed | tf_op | source)
XLA Modules:
  0.0 64.8 jit_solution(10883498694748599000)
XLA Ops:
  0.0 8.9 %local.1 = (f32[512,1024]{1,0:T(8,128)}, bf16[16,32,768]{2,1,0:T(8,128)(2,1)}, bf16[128,768]{1,0:T(8,128)(2,1)}, bf16[128,768]{1,0:T(8,128)(2,1)}, bf16[128,768]...) custom-call(s32[4]{0:T(128)} %counts_hbm.1, bf16[16,2,16,1024]{3,2,1,0:T(8,128)(2,1)} %x_hbm.1, ...), custom_call_target="tpu_custom_call" | custom-call | flops 4294967296 | bytes 12582912 | tf_op jit(solution)/shard_map/local/pallas_call | solution.py:309
  8.9 0.0 copy-start
  9.0 9.7 %all-to-all-start = ((bf16[16,32,768]{2,1,0:T(8,128)(2,1)}), bf16[16,32,768]{2,1,0:T(8,128)(2,1)S(1)}, u32[]{:S(2)}, u32[]{:S(2)}) async-start(bf16[16,32,768]{2,1,0:T(8,128)(2,1)} %get-tuple-element.17), calls=%async_computation | async-start | bytes 1572864 | tf_op jit(solution)/shard_map/all_to_all | solution.py:339
  18.7 1.5 %collective-permute-start = (bf16[128,768]{1,0:T(8,128)(2,1)}, bf16[128,768]{1,0:T(8,128)(2,1)S(1)}, u32[]{:S(2)}, u32[]{:S(2)}) collective-permute-start(bf16[128,768]{1,0:T(8,128)(2,1)} %get-tuple-element.19), channel_id=1, source_target_pairs={{0,64},{16,80},{32,96},{48,112},{64,0},{80,16},{96,32},{112,48},{1... | collective-permute-start | bytes 589832 | tf_op jit(solution)/shard_map/ppermute | solution.py:292
  20.2 2.8 %collective-permute-start.1 = (bf16[128,768]{1,0:T(8,128)(2,1)}, bf16[128,768]{1,0:T(8,128)(2,1)S(1)}, u32[]{:S(2)}, u32[]{:S(2)}) collective-permute-start(bf16[128,768]{1,0:T(8,128)(2,1)} %get-tuple-element.20), channel_id=1, source_target_pairs={{0,128},{16,144},{32,160},{48,176},{64,192},{80,208},{96,224},{112... | collective-permute-start | bytes 589832 | tf_op jit(solution)/shard_map/ppermute | solution.py:292
  23.0 0.4 collective-permute-start.2
  23.4 2.9 %collective-permute-start.3 = (bf16[128,512]{1,0:T(8,128)(2,1)}, bf16[128,512]{1,0:T(8,128)(2,1)S(1)}, u32[]{:S(2)}, u32[]{:S(2)}) collective-permute-start(bf16[128,512]{1,0:T(8,128)(2,1)} %get-tuple-element.22), channel_id=1, source_target_pairs={{0,32},{16,48},{32,0},{48,16},{64,96},{80,112},{96,64},{112,80},{1... | collective-permute-start | bytes 393224 | tf_op jit(solution)/shard_map/ppermute | solution.py:292
  26.3 0.0 collective-permute-start.7
  26.3 4.9 %collective-permute-done.3.refs_4_ = bf16[128,512]{1,0:T(8,128)(2,1)S(1)} collective-permute-done((bf16[128,512]{1,0:T(8,128)(2,1)}, bf16[128,512]{1,0:T(8,128)(2,1)S(1)}, u32[]{:S(2)}, u32[]{:S(2)}) %collective-permute-start.3) | collective-permute-done | bytes 131104 | tf_op jit(solution)/shard_map/ppermute | solution.py:292
  31.2 0.0 collective-permute-start.11
  31.2 0.0 collective-permute-done.refs_1_
  31.2 3.6 %collective-permute-start.4 = (bf16[128,512]{1,0:T(8,128)(2,1)S(1)}, bf16[128,512]{1,0:T(8,128)(2,1)S(1)}, u32[]{:S(2)}, u32[]{:S(2)}) collective-permute-start(bf16[128,512]{1,0:T(8,128)(2,1)S(1)} %slice.20), channel_id=1, source_target_pairs={{0,32},{16,48},{32,0},{48,16},{64,96},{80,112},{96,64},{112,80},{1... | collective-permute-start | bytes 393224 | tf_op jit(solution)/shard_map/ppermute | solution.py:292
  34.8 0.0 collective-permute-done.1.refs_2_
  34.9 0.1 collective-permute-start.5
  35.0 0.0 collective-permute-done.2.refs_3_
  35.0 3.6 %collective-permute-start.6 = (bf16[128,512]{1,0:T(8,128)(2,1)S(1)}, bf16[128,512]{1,0:T(8,128)(2,1)S(1)}, u32[]{:S(2)}, u32[]{:S(2)}) collective-permute-start(bf16[128,512]{1,0:T(8,128)(2,1)S(1)} %slice.22), channel_id=1, source_target_pairs={{0,32},{16,48},{32,0},{48,16},{64,96},{80,112},{96,64},{112,80},{1... | collective-permute-start | bytes 393224 | tf_op jit(solution)/shard_map/ppermute | solution.py:292
  38.6 0.0 collective-permute-done.7.refs_8_
  38.6 0.0 collective-permute-start.10
  38.6 0.9 %all-to-all-done.x_ref = bf16[16,32,768]{2,1,0:T(8,128)(2,1)S(1)} async-done(((bf16[16,32,768]{2,1,0:T(8,128)(2,1)}), bf16[16,32,768]{2,1,0:T(8,128)(2,1)S(1)}, u32[]{:S(2)}, u32[]{:S(2)}) %all-to-all-start) | async-done | bytes 786464 | tf_op jit(solution)/shard_map/all_to_all | solution.py:339
  39.5 2.4 %row_attention.1 = bf16[16,32,256]{2,1,0:T(8,128)(2,1)} custom-call(bf16[16,32,768]{2,1,0:T(8,128)(2,1)S(1)} %all-to-all-done.x_ref), custom_call_target="tpu_custom_call" | custom-call | flops 536870912 | bytes 1048576 | tf_op jit(solution)/shard_map/row_attention/pallas_call | solution.py:349
  41.9 8.0 %all-to-all-start.1 = ((bf16[16,32,256]{2,1,0:T(8,128)(2,1)}), bf16[16,32,256]{2,1,0:T(8,128)(2,1)S(1)}, u32[]{:S(2)}, u32[]{:S(2)}) async-start(bf16[16,32,256]{2,1,0:T(8,128)(2,1)} %row_attention.1), calls=%async_computation.1 | async-start | bytes 524288 | tf_op jit(solution)/shard_map/all_to_all | solution.py:358
  49.9 0.0 collective-permute-done.11.refs_12_
  49.9 0.1 collective-permute-start.8
  50.0 0.0 collective-permute-done.4.refs_5_
  50.0 0.5 collective-permute-start.9
  50.5 0.0 collective-permute-done.5.refs_6_
  50.5 0.1 collective-permute-start.12
  50.6 0.0 collective-permute-done.6.refs_7_
  50.6 0.4 collective-permute-start.13
  51.0 0.0 collective-permute-done.10.refs_11_
  51.0 0.1 collective-permute-start.14
  51.1 0.2 collective-permute-done.8.refs_9_
  51.3 0.2 collective-permute-done.9.refs_10_
  51.5 0.3 collective-permute-done.12.refs_13_
  51.8 0.2 collective-permute-done.13.refs_14_
  52.0 0.3 collective-permute-done.14.refs_15_
  52.4 0.0 copy-done
  52.4 0.9 %column_attention.1 = (bf16[128,256]{1,0:T(8,128)(2,1)S(1)}, bf16[128,256]{1,0:T(8,128)(2,1)S(1)}, bf16[128,256]{1,0:T(8,128)(2,1)S(1)}, bf16[128,256]{1,0:T(8,128)(2,1)S(1)}) custom-call(bf16[128,768]{1,0:T(8,128)(2,1)S(1)} %copy-done, bf16[128,768]{1,0:T(8,128)(2,1)S(1)} %collective-permute-done.refs_1_, ...), custom_call_target="tpu_custom_call" | custom-call | flops 268435456 | bytes 1048576 | tf_op jit(solution)/shard_map/column_attention/pallas_call | solution.py:359
  53.3 0.1 collective-permute-start.15
  53.4 4.2 %collective-permute-start.16 = (bf16[128,256]{1,0:T(8,128)(2,1)S(1)}, bf16[128,256]{1,0:T(8,128)(2,1)S(1)}, u32[]{:S(2)}, u32[]{:S(2)}) collective-permute-start(bf16[128,256]{1,0:T(8,128)(2,1)S(1)} %get-tuple-element.25), channel_id=1, source_target_pairs={{0,128},{16,144},{32,160},{48,176},{64,192},{80,208},{96,224},{112... | collective-permute-start | bytes 196616 | tf_op jit(solution)/shard_map/ppermute | solution.py:292
  57.6 0.4 collective-permute-start.17
  58.1 1.3 %fusion = (bf16[256,1024]{1,0:T(8,128)(2,1)S(1)}, bf16[256,1024]{1,0:T(8,128)(2,1)S(1)}) fusion(bf16[512,1024]{1,0:T(8,128)(2,1)} %param.15), kind=kLoop, calls=%fused_computation | loop fusion | bytes 2097152 | tf_op jit(solution)/shard_map/slice | solution.py:393
  59.3 1.3 %all-to-all-done.1.row_ref = bf16[16,32,256]{2,1,0:T(8,128)(2,1)S(1)} async-done(((bf16[16,32,256]{2,1,0:T(8,128)(2,1)}), bf16[16,32,256]{2,1,0:T(8,128)(2,1)S(1)}, u32[]{:S(2)}, u32[]{:S(2)}) %all-to-all-start.1) | async-done | bytes 262176 | tf_op jit(solution)/shard_map/all_to_all | solution.py:358
  60.6 2.0 %row_projection.1.acc_ref = f32[512,1024]{1,0:T(8,128)S(1)} custom-call(f32[512,1024]{1,0:T(8,128)} %get-tuple-element.16.resid_hbm, bf16[16,32,256]{2,1,0:T(8,128)(2,1)S(1)} %all-to-all-done.1.row_ref, bf16[256,1024]{1,0:T(8,128)(2,1)S(1)} %get-tuple-element.28.w_ref), custom_call_target="tpu_custom_call" | custom-call | flops 268435456 | bytes 5242880 | tf_op jit(solution)/shard_map/row_projection/pallas_call | solution.py:371
  62.7 0.0 collective-permute-done.15.p1
  62.7 0.0 collective-permute-done.16.p2
  62.7 0.4 collective-permute-done.17.p3
  63.1 1.5 %column_projection.1 = bf16[512,1024]{1,0:T(8,128)(2,1)} custom-call(s32[1]{0:T(128)} %bitcast.me_ref, f32[512,1024]{1,0:T(8,128)S(1)} %row_projection.1.acc_ref, bf16[128,256]{1,0:T(8,128)(2,1)S(1)} %get-tuple-element.23.p0, bf16[128,256]{1,0:T(8,128)(2,1)S(1)} %collective-permute-done.15.p1, bf16[128,256]{1,0:T(8,128)(2,1)S(1)} %collective-permute-done.16.p2, ...), custom_call_target="tpu_custom_call" | custom-call | flops 268435456 | bytes 5242880 | tf_op jit(solution)/shard_map/column_projection/pallas_call | solution.py:380
  (3 shorter events, 0.0 us)
Async XLA Ops:
  8.9 43.4 %copy-start = (bf16[128,768]{1,0:T(8,128)(2,1)S(1)}, bf16[128,768]{1,0:T(8,128)(2,1)}, u32[]{:S(2)}) copy-start(bf16[128,768]{1,0:T(8,128)(2,1)} %get-tuple-element.18.refs_0_) | copy-start | bytes 589828
  9.0 30.5 %all-to-all-start = ((bf16[16,32,768]{2,1,0:T(8,128)(2,1)}), bf16[16,32,768]{2,1,0:T(8,128)(2,1)S(1)}, u32[]{:S(2)}, u32[]{:S(2)}) async-start(bf16[16,32,768]{2,1,0:T(8,128)(2,1)} %get-tuple-element.17), calls=%async_computation | async-start | bytes 1572864 | tf_op jit(solution)/shard_map/all_to_all | solution.py:339
  18.7 12.5 %collective-permute-start = (bf16[128,768]{1,0:T(8,128)(2,1)}, bf16[128,768]{1,0:T(8,128)(2,1)S(1)}, u32[]{:S(2)}, u32[]{:S(2)}) collective-permute-start(bf16[128,768]{1,0:T(8,128)(2,1)} %get-tuple-element.19), channel_id=1, source_target_pairs={{0,64},{16,80},{32,96},{48,112},{64,0},{80,16},{96,32},{112,48},{1... | collective-permute-start | bytes 589832 | tf_op jit(solution)/shard_map/ppermute | solution.py:292
  20.2 14.7 %collective-permute-start.1 = (bf16[128,768]{1,0:T(8,128)(2,1)}, bf16[128,768]{1,0:T(8,128)(2,1)S(1)}, u32[]{:S(2)}, u32[]{:S(2)}) collective-permute-start(bf16[128,768]{1,0:T(8,128)(2,1)} %get-tuple-element.20), channel_id=1, source_target_pairs={{0,128},{16,144},{32,160},{48,176},{64,192},{80,208},{96,224},{112... | collective-permute-start | bytes 589832 | tf_op jit(solution)/shard_map/ppermute | solution.py:292
  23.0 12.0 %collective-permute-start.2 = (bf16[128,768]{1,0:T(8,128)(2,1)}, bf16[128,768]{1,0:T(8,128)(2,1)S(1)}, u32[]{:S(2)}, u32[]{:S(2)}) collective-permute-start(bf16[128,768]{1,0:T(8,128)(2,1)} %get-tuple-element.21), channel_id=1, source_target_pairs={{0,192},{16,208},{32,224},{48,240},{64,128},{80,144},{96,160},{112... | collective-permute-start | bytes 589832 | tf_op jit(solution)/shard_map/ppermute | solution.py:292
  23.4 7.8 %collective-permute-start.3 = (bf16[128,512]{1,0:T(8,128)(2,1)}, bf16[128,512]{1,0:T(8,128)(2,1)S(1)}, u32[]{:S(2)}, u32[]{:S(2)}) collective-permute-start(bf16[128,512]{1,0:T(8,128)(2,1)} %get-tuple-element.22), channel_id=1, source_target_pairs={{0,32},{16,48},{32,0},{48,16},{64,96},{80,112},{96,64},{112,80},{1... | collective-permute-start | bytes 393224 | tf_op jit(solution)/shard_map/ppermute | solution.py:292
  26.3 12.3 %collective-permute-start.7 = (bf16[128,512]{1,0:T(8,128)(2,1)}, bf16[128,512]{1,0:T(8,128)(2,1)S(1)}, u32[]{:S(2)}, u32[]{:S(2)}) collective-permute-start(bf16[128,512]{1,0:T(8,128)(2,1)} %get-tuple-element.22), channel_id=1, source_target_pairs={{0,16},{16,0},{32,48},{48,32},{64,80},{80,64},{96,112},{112,96},{1... | collective-permute-start | bytes 393224 | tf_op jit(solution)/shard_map/ppermute | solution.py:292
  31.2 18.7 %collective-permute-start.11 = (bf16[128,512]{1,0:T(8,128)(2,1)S(1)}, bf16[128,512]{1,0:T(8,128)(2,1)S(1)}, u32[]{:S(2)}, u32[]{:S(2)}) collective-permute-start(bf16[128,512]{1,0:T(8,128)(2,1)S(1)} %collective-permute-done.3.refs_4_), channel_id=1, source_target_pairs={{0,16},{16,0},{32,48},{48,32},{64,80},{80,64},{96,112},{112,96},{1... | collective-permute-start | bytes 393224 | tf_op jit(solution)/shard_map/ppermute | solution.py:292
  31.2 18.8 %collective-permute-start.4 = (bf16[128,512]{1,0:T(8,128)(2,1)S(1)}, bf16[128,512]{1,0:T(8,128)(2,1)S(1)}, u32[]{:S(2)}, u32[]{:S(2)}) collective-permute-start(bf16[128,512]{1,0:T(8,128)(2,1)S(1)} %slice.20), channel_id=1, source_target_pairs={{0,32},{16,48},{32,0},{48,16},{64,96},{80,112},{96,64},{112,80},{1... | collective-permute-start | bytes 393224 | tf_op jit(solution)/shard_map/ppermute | solution.py:292
  34.9 15.6 %collective-permute-start.5 = (bf16[128,512]{1,0:T(8,128)(2,1)S(1)}, bf16[128,512]{1,0:T(8,128)(2,1)S(1)}, u32[]{:S(2)}, u32[]{:S(2)}) collective-permute-start(bf16[128,512]{1,0:T(8,128)(2,1)S(1)} %slice.21), channel_id=1, source_target_pairs={{0,32},{16,48},{32,0},{48,16},{64,96},{80,112},{96,64},{112,80},{1... | collective-permute-start | bytes 393224 | tf_op jit(solution)/shard_map/ppermute | solution.py:292
  35.0 15.6 %collective-permute-start.6 = (bf16[128,512]{1,0:T(8,128)(2,1)S(1)}, bf16[128,512]{1,0:T(8,128)(2,1)S(1)}, u32[]{:S(2)}, u32[]{:S(2)}) collective-permute-start(bf16[128,512]{1,0:T(8,128)(2,1)S(1)} %slice.22), channel_id=1, source_target_pairs={{0,32},{16,48},{32,0},{48,16},{64,96},{80,112},{96,64},{112,80},{1... | collective-permute-start | bytes 393224 | tf_op jit(solution)/shard_map/ppermute | solution.py:292
  38.6 12.4 %collective-permute-start.10 = (bf16[128,512]{1,0:T(8,128)(2,1)S(1)}, bf16[128,512]{1,0:T(8,128)(2,1)S(1)}, u32[]{:S(2)}, u32[]{:S(2)}) collective-permute-start(bf16[128,512]{1,0:T(8,128)(2,1)S(1)} %slice.22), channel_id=1, source_target_pairs={{0,16},{16,0},{32,48},{48,32},{64,80},{80,64},{96,112},{112,96},{1... | collective-permute-start | bytes 393224 | tf_op jit(solution)/shard_map/ppermute | solution.py:292
  41.9 18.8 %all-to-all-start.1 = ((bf16[16,32,256]{2,1,0:T(8,128)(2,1)}), bf16[16,32,256]{2,1,0:T(8,128)(2,1)S(1)}, u32[]{:S(2)}, u32[]{:S(2)}) async-start(bf16[16,32,256]{2,1,0:T(8,128)(2,1)} %row_attention.1), calls=%async_computation.1 | async-start | bytes 524288 | tf_op jit(solution)/shard_map/all_to_all | solution.py:358
  49.9 1.4 %collective-permute-start.8 = (bf16[128,512]{1,0:T(8,128)(2,1)S(1)}, bf16[128,512]{1,0:T(8,128)(2,1)S(1)}, u32[]{:S(2)}, u32[]{:S(2)}) collective-permute-start(bf16[128,512]{1,0:T(8,128)(2,1)S(1)} %slice.20), channel_id=1, source_target_pairs={{0,16},{16,0},{32,48},{48,32},{64,80},{80,64},{96,112},{112,96},{1... | collective-permute-start | bytes 393224 | tf_op jit(solution)/shard_map/ppermute | solution.py:292
  50.0 1.5 %collective-permute-start.9 = (bf16[128,512]{1,0:T(8,128)(2,1)S(1)}, bf16[128,512]{1,0:T(8,128)(2,1)S(1)}, u32[]{:S(2)}, u32[]{:S(2)}) collective-permute-start(bf16[128,512]{1,0:T(8,128)(2,1)S(1)} %slice.21), channel_id=1, source_target_pairs={{0,16},{16,0},{32,48},{48,32},{64,80},{80,64},{96,112},{112,96},{1... | collective-permute-start | bytes 393224 | tf_op jit(solution)/shard_map/ppermute | solution.py:292
  50.5 1.3 %collective-permute-start.12 = (bf16[128,512]{1,0:T(8,128)(2,1)S(1)}, bf16[128,512]{1,0:T(8,128)(2,1)S(1)}, u32[]{:S(2)}, u32[]{:S(2)}) collective-permute-start(bf16[128,512]{1,0:T(8,128)(2,1)S(1)} %collective-permute-done.4.refs_5_), channel_id=1, source_target_pairs={{0,16},{16,0},{32,48},{48,32},{64,80},{80,64},{96,112},{112,96},{1... | collective-permute-start | bytes 393224 | tf_op jit(solution)/shard_map/ppermute | solution.py:292
  50.6 1.4 %collective-permute-start.13 = (bf16[128,512]{1,0:T(8,128)(2,1)S(1)}, bf16[128,512]{1,0:T(8,128)(2,1)S(1)}, u32[]{:S(2)}, u32[]{:S(2)}) collective-permute-start(bf16[128,512]{1,0:T(8,128)(2,1)S(1)} %collective-permute-done.5.refs_6_), channel_id=1, source_target_pairs={{0,16},{16,0},{32,48},{48,32},{64,80},{80,64},{96,112},{112,96},{1... | collective-permute-start | bytes 393224 | tf_op jit(solution)/shard_map/ppermute | solution.py:292
  51.0 1.3 %collective-permute-start.14 = (bf16[128,512]{1,0:T(8,128)(2,1)S(1)}, bf16[128,512]{1,0:T(8,128)(2,1)S(1)}, u32[]{:S(2)}, u32[]{:S(2)}) collective-permute-start(bf16[128,512]{1,0:T(8,128)(2,1)S(1)} %collective-permute-done.6.refs_7_), channel_id=1, source_target_pairs={{0,16},{16,0},{32,48},{48,32},{64,80},{80,64},{96,112},{112,96},{1... | collective-permute-start | bytes 393224 | tf_op jit(solution)/shard_map/ppermute | solution.py:292
  53.3 9.4 %collective-permute-start.15 = (bf16[128,256]{1,0:T(8,128)(2,1)S(1)}, bf16[128,256]{1,0:T(8,128)(2,1)S(1)}, u32[]{:S(2)}, u32[]{:S(2)}) collective-permute-start(bf16[128,256]{1,0:T(8,128)(2,1)S(1)} %get-tuple-element.24), channel_id=1, source_target_pairs={{0,64},{16,80},{32,96},{48,112},{64,0},{80,16},{96,32},{112,48},{1... | collective-permute-start | bytes 196616 | tf_op jit(solution)/shard_map/ppermute | solution.py:292
  53.4 9.3 %collective-permute-start.16 = (bf16[128,256]{1,0:T(8,128)(2,1)S(1)}, bf16[128,256]{1,0:T(8,128)(2,1)S(1)}, u32[]{:S(2)}, u32[]{:S(2)}) collective-permute-start(bf16[128,256]{1,0:T(8,128)(2,1)S(1)} %get-tuple-element.25), channel_id=1, source_target_pairs={{0,128},{16,144},{32,160},{48,176},{64,192},{80,208},{96,224},{112... | collective-permute-start | bytes 196616 | tf_op jit(solution)/shard_map/ppermute | solution.py:292
  57.6 5.5 %collective-permute-start.17 = (bf16[128,256]{1,0:T(8,128)(2,1)S(1)}, bf16[128,256]{1,0:T(8,128)(2,1)S(1)}, u32[]{:S(2)}, u32[]{:S(2)}) collective-permute-start(bf16[128,256]{1,0:T(8,128)(2,1)S(1)} %get-tuple-element.26), channel_id=1, source_target_pairs={{0,192},{16,208},{32,224},{48,240},{64,128},{80,144},{96,160},{112... | collective-permute-start | bytes 196616 | tf_op jit(solution)/shard_map/ppermute | solution.py:292
